TPU v7x, 256 devices: a whole 4x4x8 slice. The times are simulated.
256 devices in a mesh: grp: 4 (over x), tp: 32 (over z, y), srv: 2 (over core).
Axes of the slice: x: 4, y: 4, z: 8, core: 2. Of those that a mesh axis runs over, the one named last changes fastest.
Arguments:
- tokens: bfloat16 [32768, 2048], P(('grp', 'tp', 'srv')), may hold values from -100 to 100
- norm_gain: float32 [2048], replicated, may hold values from 0.1 to 1.9
- query_weight: bfloat16 [2048, 4096], P(None, 'srv'), may hold values from -0.125 to 0.125
- key_matrix: bfloat16 [2048, 512], P(None, 'srv'), may hold values from -0.125 to 0.125
- value_matrix: bfloat16 [2048, 512], P(None, 'srv'), may hold values from -0.125 to 0.125
- query_gain: float32 [128], replicated, may hold values from 1.2 to 2.2
- key_gain: float32 [128], replicated, may hold values from 1.2 to 2.2
- lengths: int32 [32], replicated, may hold values from 1 to 4096, as said below
Outputs:
- attended: bfloat16 [32768, 4096], P(('grp', 'tp'), 'srv')
Inputs may be any that keep to these rules, and one draw needn't show every extreme that they name: 32 document lengths in the order in which the documents are packed; they sum to 32768, the second to last of them is exactly 4096 and the last is 128.
All inputs are finite; a program needn't handle non-finite values.
Results may differ from a plain program's by a relative error of at most 0.012.
Values may be sent and summed in bfloat16 or wider, within the bound.
No kernel may reach another device: no remote copies, remote signals or barrier semaphores. Data moves between devices by JAX's collectives and lax.ppermute only.
A program may use at most 128 MiB of HBM per device.

v0:
```python
import math

import jax
import jax.numpy as jnp
from jax import lax
from jax.sharding import PartitionSpec as P

EPSILON = 1e-06
THETA = 1000000.0


def sent_to_all(x, axis):
    length = lax.axis_size(axis)
    return lax.all_to_all(jnp.broadcast_to(x[None], (length, *x.shape)), axis, 0, 0, tiled=True)


def in_order(parts, dim):
    dims = list(parts.shape[1:])
    dims[dim] *= parts.shape[0]
    return jnp.moveaxis(parts, 0, dim).reshape(dims)


def gathered_copies(x, axis, dim):
    parts = sent_to_all(x, axis)
    return in_order(parts, dim)


def from_behind(x, axis, by):
    length = lax.axis_size(axis)
    pairs = [(i, i + by) for i in range(length) if 0 <= i + by < length]
    return lax.ppermute(x, axis, pairs)


def head_norm(value_rows, factor):
    scaled = value_rows * lax.rsqrt(
        jnp.mean(value_rows * value_rows, axis=-1, keepdims=True) + EPSILON
    )
    return scaled * factor


def rotate(value_rows, offsets):
    halfway = value_rows.shape[-1] // 2
    inverse = jnp.exp(
        -(2.0 * jnp.arange(halfway, dtype=jnp.float32) / value_rows.shape[-1]) * math.log(THETA)
    )
    angles = offsets.astype(jnp.float32)[:, None] * inverse[None, :]
    cosine = jnp.cos(angles)[:, None, :]
    sinusoid = jnp.sin(angles)[:, None, :]
    former = value_rows[..., :halfway]
    latter = value_rows[..., halfway:]
    return jnp.concatenate(
        [former * cosine - latter * sinusoid, latter * cosine + former * sinusoid], axis=-1
    )


def doc_bounds(positions, lengths):
    finish = jnp.cumsum(lengths)
    before = positions[:, None] >= finish[None, :]
    number = jnp.sum(before.astype(jnp.int32), axis=1)
    opening = jnp.max(jnp.where(before, finish[None, :], jnp.zeros_like(finish)[None, :]), axis=1)
    return (number, opening)


def per_device(
    tokens, norm_gain, query_weight, key_matrix, value_matrix, query_gain, key_gain, lengths
):
    chip_rows = gathered_copies(tokens, "srv", 0)
    row_count = chip_rows.shape[0]
    head_dim = query_gain.shape[0]
    pair_width = key_matrix.shape[1]
    key_heads = pair_width // head_dim
    query_heads = query_weight.shape[1] // head_dim
    groups = query_heads // key_heads
    projectors = lax.axis_size("grp") * lax.axis_size("tp")
    reach_shards = min(16, projectors // 2)
    shard_index = lax.axis_index("grp") * lax.axis_size("tp") + lax.axis_index("tp")
    first_row = shard_index * row_count
    positions = first_row + jnp.arange(row_count, dtype=jnp.int32)
    query_doc, query_open = doc_bounds(positions, lengths)
    offsets = positions - query_open
    floated = chip_rows.astype(jnp.float32)
    normalized_rows = (
        floated
        * lax.rsqrt(jnp.mean(floated * floated, axis=-1, keepdims=True) + EPSILON)
        * norm_gain
    ).astype(jnp.bfloat16)
    unnormed_keys = jnp.dot(
        normalized_rows, key_matrix, preferred_element_type=jnp.float32
    ).reshape(row_count, key_heads, head_dim)
    key_rows = (
        rotate(head_norm(unnormed_keys, key_gain), offsets)
        .astype(jnp.bfloat16)
        .reshape(row_count, pair_width)
    )
    value_rows = jnp.dot(normalized_rows, value_matrix, preferred_element_type=jnp.float32).astype(
        jnp.bfloat16
    )
    stacked = jnp.stack([key_rows, value_rows], 0)
    span_count = reach_shards + 2
    window = stacked
    covered = 1
    for bit_index in range(span_count.bit_length() - 2, -1, -1):
        window = jnp.concatenate([from_behind(window, ("grp", "tp"), covered), window], 1)
        covered = covered * 2
        if span_count >> bit_index & 1:
            window = jnp.concatenate([from_behind(stacked, ("grp", "tp"), covered), window], 1)
            covered = covered + 1
    window_start = (shard_index - covered + 1) * row_count
    query_raw = jnp.dot(normalized_rows, query_weight, preferred_element_type=jnp.float32).reshape(
        row_count, query_heads, head_dim
    )
    query_rows = rotate(head_norm(query_raw, query_gain), offsets).astype(jnp.bfloat16)
    query_rows = query_rows.reshape(row_count, key_heads, groups, head_dim)
    key_span = 512
    lowest = jnp.maximum(query_open[0] - window_start, 0) // key_span
    highest = (first_row + row_count - 1 - window_start) // key_span + 1
    scaling = head_dim ** (-0.5)

    def attend_block(block_index, running):
        accumulated, denominator = running
        block_start = block_index * key_span
        block_pair = lax.dynamic_slice_in_dim(window, block_start, key_span, 1)
        key_block = block_pair[0].reshape(key_span, key_heads, head_dim)
        value_block = block_pair[1].reshape(key_span, key_heads, head_dim)
        key_pos = window_start + block_start + jnp.arange(key_span, dtype=jnp.int32)
        key_doc, unused_open = doc_bounds(key_pos, lengths)
        allowed = (
            (key_doc[None, :] == query_doc[:, None])
            & (key_pos[None, :] <= positions[:, None])
            & (key_pos >= 0)[None, :]
        )
        scores = (
            jnp.einsum("thgd,khd->thgk", query_rows, key_block, preferred_element_type=jnp.float32)
            * scaling
        )
        weights = jnp.where(allowed[:, None, None, :], jnp.exp(scores), 0.0)
        denominator = denominator + jnp.sum(weights, axis=-1)
        accumulated = accumulated + jnp.einsum(
            "thgk,khd->thgd",
            weights.astype(jnp.bfloat16),
            value_block,
            preferred_element_type=jnp.float32,
        )
        return (accumulated, denominator)

    starting_state = (
        jnp.zeros((row_count, key_heads, groups, head_dim), jnp.float32),
        jnp.zeros((row_count, key_heads, groups), jnp.float32),
    )
    accumulated, denominator = lax.fori_loop(lowest, highest, attend_block, starting_state)
    return (
        (accumulated / denominator[..., None])
        .reshape(row_count, query_heads * head_dim)
        .astype(jnp.bfloat16)
    )


def solution(mesh):
    placed = (
        P(("grp", "tp", "srv"), None),
        P(),
        P(None, "srv"),
        P(None, "srv"),
        P(None, "srv"),
        P(),
        P(),
        P(),
    )
    return jax.shard_map(
        per_device, mesh=mesh, in_specs=placed, out_specs=P(("grp", "tp"), "srv"), check_vma=False
    )
```

profile of v0, /device:TPU:255, one launch (start us, length us, event | category | flops | bytes accessed | tf_op | source)
XLA Modules:
  0.0 300.6 jit_solution(4627264183650973073)
XLA Ops:
  0.0 2.2 broadcast_in_dim.41
  2.2 4.4 %all-to-all-start = ((bf16[2,128,2048]{2,1,0:T(8,128)(2,1)}), bf16[2,128,2048]{2,1,0:T(8,128)(2,1)S(1)}, u32[]{:S(2)}, u32[]{:S(2)}) async-start(bf16[2,128,2048]{2,1,0:T(8,128)(2,1)} %broadcast_in_dim.41), calls=%async_computation | async-start | bytes 2097152 | tf_op jit(solution)/shard_map/all_to_all | solution.py:14
  7.4 1.3 fusion.17
  9.0 1.5 copy.38
  13.3 1.3 collective-permute-start.1
  14.6 8.4 %collective-permute-done.1 = bf16[2,256,256]{2,1,0:T(8,128)(2,1)S(1)} collective-permute-done((bf16[2,256,256]{2,1,0:T(8,128)(2,1)S(1)}, bf16[2,256,256]{2,1,0:T(8,128)(2,1)S(1)}, u32[]{:S(2)}, u32[]{:S(2)}) %collective-permute-start.1) | collective-permute-done | bytes 262176 | tf_op jit(solution)/shard_map/ppermute | solution.py:31
  23.1 1.3 collective-permute-start.2
  24.4 14.7 %collective-permute-done.2 = bf16[2,512,256]{2,1,0:T(8,128)(2,1)S(1)} collective-permute-done((bf16[2,512,256]{2,1,0:T(8,128)(2,1)S(1)}, bf16[2,512,256]{2,1,0:T(8,128)(2,1)S(1)}, u32[]{:S(2)}, u32[]{:S(2)}) %collective-permute-start.2) | collective-permute-done | bytes 524320 | tf_op jit(solution)/shard_map/ppermute | solution.py:31
  39.1 1.3 collective-permute-start.3
  40.4 1.3 collective-permute-start
  41.7 34.0 %collective-permute-done = bf16[2,256,256]{2,1,0:T(8,128)(2,1)S(1)} collective-permute-done((bf16[2,256,256]{2,1,0:T(8,128)(2,1)S(1)}, bf16[2,256,256]{2,1,0:T(8,128)(2,1)S(1)}, u32[]{:S(2)}, u32[]{:S(2)}) %collective-permute-start) | collective-permute-done | bytes 262176 | tf_op jit(solution)/shard_map/ppermute | solution.py:31
  80.7 1.3 collective-permute-start.4
  83.2 12.4 %copy.39 = bf16[2048,2048]{1,0:T(8,128)(2,1)} copy(bf16[2048,2048]{0,1:T(8,128)(2,1)} %bitcast.74) | data formatting | bytes 16777216 | tf_op jit(solution)/shard_map/dot_general | solution.py:109
  95.5 5.8 %multiply_reduce_fusion = (f32[256,16]{0,1:T(8,128)S(1)}, f32[256,16,128]{0,2,1:T(8,128)S(1)}) fusion(bf16[256,2048,1]{1,0,2:T(8,128)(2,1)S(1)} %bitcast.80, bf16[16,128,2048]{2,1,0:T(8,128)(2,1)} %bitcast.75), kind=kOutput, calls=%fused_computation.23 | convolution fusion | flops 2148528128 | bytes 11550720 | tf_op jit(solution)/shard_map/dot_general | solution.py:109
  102.2 1.3 subtract_convert_fusion
  103.5 1.5 copy.32
  105.0 2.4 copy.31
  107.4 2.8 pad_maximum_fusion
  110.3 77.2 %collective-permute-done.4 = bf16[2,2304,256]{2,1,0:T(8,128)(2,1)} collective-permute-done((bf16[2,2304,256]{2,1,0:T(8,128)(2,1)}, bf16[2,2304,256]{2,1,0:T(8,128)(2,1)}, u32[]{:S(2)}, u32[]{:S(2)}) %collective-permute-start.4) | collective-permute-done | bytes 2359328 | tf_op jit(solution)/shard_map/ppermute | solution.py:31
  187.5 1.8 constant_dynamic-update-slice_fusion.10
  189.8 1.9 copy-done.1
  191.7 105.5 %while.15 = (s32[]{:T(128)}, f32[256,2,8,128]{0,3,2,1:T(8,128)S(1)}, f32[256,2,8]{0,2,1:T(8,128)S(1)}, s32[]{:T(128)}, bf16[2,4608,256]{2,1,0:T(8,128)(2,1)}, /*...) while((s32[]{:T(128)}, ...), condition=%wide.region_9.10_spmd.clone, body=%wide.region_6.9_spmd.clone.sunk | while | flops 1087423744 | bytes 25114984 | solution.py:150
  193.4 1.9 constant_dynamic-slice_fusion.3
  195.3 1.1 copy.48
  196.4 1.8 copy.49
  198.1 3.3 %fusion.37 = (f32[256,2,8]{0,2,1:T(8,128)S(1)}, f32[2,512,256,8]{2,1,3,0:T(8,128)S(1)}) fusion(pred[256,512]{0,1:T(8,128)(4,1)S(1)} %and_and_fusion.2, bf16[512,2,128,1]{0,2,3,1:T(8,128)(2,1)} %bitcast.76, bf16[256,2,8,128]{3,0,2,1:T(8,128)(2,1)} %get-tuple-element.327), kind=kOutput, calls=%fused_computation.2.clone.1 | convolution fusion | flops 543158272 | bytes 9846784 | tf_op jit(solution)/shard_map/while/body/thgd,khd->thgk/dot_general | solution.py:133
  201.5 1.9 bitcast_add_fusion.2
  205.1 1.9 constant_dynamic-slice_fusion.3
  207.0 1.1 copy.48
  208.1 1.8 copy.49
  209.9 3.3 %fusion.37 = (f32[256,2,8]{0,2,1:T(8,128)S(1)}, f32[2,512,256,8]{2,1,3,0:T(8,128)S(1)}) fusion(pred[256,512]{0,1:T(8,128)(4,1)S(1)} %and_and_fusion.2, bf16[512,2,128,1]{0,2,3,1:T(8,128)(2,1)} %bitcast.76, bf16[256,2,8,128]{3,0,2,1:T(8,128)(2,1)} %get-tuple-element.327), kind=kOutput, calls=%fused_computation.2.clone.1 | convolution fusion | flops 543158272 | bytes 9846784 | tf_op jit(solution)/shard_map/while/body/thgd,khd->thgk/dot_general | solution.py:133
  213.2 1.9 bitcast_add_fusion.2
  216.8 1.9 constant_dynamic-slice_fusion.3
  218.7 1.1 copy.48
  219.8 1.8 copy.49
  221.6 3.3 %fusion.37 = (f32[256,2,8]{0,2,1:T(8,128)S(1)}, f32[2,512,256,8]{2,1,3,0:T(8,128)S(1)}) fusion(pred[256,512]{0,1:T(8,128)(4,1)S(1)} %and_and_fusion.2, bf16[512,2,128,1]{0,2,3,1:T(8,128)(2,1)} %bitcast.76, bf16[256,2,8,128]{3,0,2,1:T(8,128)(2,1)} %get-tuple-element.327), kind=kOutput, calls=%fused_computation.2.clone.1 | convolution fusion | flops 543158272 | bytes 9846784 | tf_op jit(solution)/shard_map/while/body/thgd,khd->thgk/dot_general | solution.py:133
  224.9 1.9 bitcast_add_fusion.2
  228.6 1.9 constant_dynamic-slice_fusion.3
  231.5 1.8 copy.49
  233.3 3.3 %fusion.37 = (f32[256,2,8]{0,2,1:T(8,128)S(1)}, f32[2,512,256,8]{2,1,3,0:T(8,128)S(1)}) fusion(pred[256,512]{0,1:T(8,128)(4,1)S(1)} %and_and_fusion.2, bf16[512,2,128,1]{0,2,3,1:T(8,128)(2,1)} %bitcast.76, bf16[256,2,8,128]{3,0,2,1:T(8,128)(2,1)} %get-tuple-element.327), kind=kOutput, calls=%fused_computation.2.clone.1 | convolution fusion | flops 543158272 | bytes 9846784 | tf_op jit(solution)/shard_map/while/body/thgd,khd->thgk/dot_general | solution.py:133
  236.6 1.9 bitcast_add_fusion.2
  240.3 1.9 constant_dynamic-slice_fusion.3
  243.2 1.8 copy.49
  245.0 3.3 %fusion.37 = (f32[256,2,8]{0,2,1:T(8,128)S(1)}, f32[2,512,256,8]{2,1,3,0:T(8,128)S(1)}) fusion(pred[256,512]{0,1:T(8,128)(4,1)S(1)} %and_and_fusion.2, bf16[512,2,128,1]{0,2,3,1:T(8,128)(2,1)} %bitcast.76, bf16[256,2,8,128]{3,0,2,1:T(8,128)(2,1)} %get-tuple-element.327), kind=kOutput, calls=%fused_computation.2.clone.1 | convolution fusion | flops 543158272 | bytes 9846784 | tf_op jit(solution)/shard_map/while/body/thgd,khd->thgk/dot_general | solution.py:133
  248.3 1.9 bitcast_add_fusion.2
  252.0 1.9 constant_dynamic-slice_fusion.3
  253.9 1.1 copy.48
  255.0 1.8 copy.49
  256.7 3.3 %fusion.37 = (f32[256,2,8]{0,2,1:T(8,128)S(1)}, f32[2,512,256,8]{2,1,3,0:T(8,128)S(1)}) fusion(pred[256,512]{0,1:T(8,128)(4,1)S(1)} %and_and_fusion.2, bf16[512,2,128,1]{0,2,3,1:T(8,128)(2,1)} %bitcast.76, bf16[256,2,8,128]{3,0,2,1:T(8,128)(2,1)} %get-tuple-element.327), kind=kOutput, calls=%fused_computation.2.clone.1 | convolution fusion | flops 543158272 | bytes 9846784 | tf_op jit(solution)/shard_map/while/body/thgd,khd->thgk/dot_general | solution.py:133
  260.1 1.9 bitcast_add_fusion.2
  263.7 1.9 constant_dynamic-slice_fusion.3
  266.7 1.8 copy.49
  268.5 3.3 %fusion.37 = (f32[256,2,8]{0,2,1:T(8,128)S(1)}, f32[2,512,256,8]{2,1,3,0:T(8,128)S(1)}) fusion(pred[256,512]{0,1:T(8,128)(4,1)S(1)} %and_and_fusion.2, bf16[512,2,128,1]{0,2,3,1:T(8,128)(2,1)} %bitcast.76, bf16[256,2,8,128]{3,0,2,1:T(8,128)(2,1)} %get-tuple-element.327), kind=kOutput, calls=%fused_computation.2.clone.1 | convolution fusion | flops 543158272 | bytes 9846784 | tf_op jit(solution)/shard_map/while/body/thgd,khd->thgk/dot_general | solution.py:133
  271.8 1.9 bitcast_add_fusion.2
  275.5 1.9 constant_dynamic-slice_fusion.3
  278.4 1.8 copy.49
  280.2 3.3 %fusion.37 = (f32[256,2,8]{0,2,1:T(8,128)S(1)}, f32[2,512,256,8]{2,1,3,0:T(8,128)S(1)}) fusion(pred[256,512]{0,1:T(8,128)(4,1)S(1)} %and_and_fusion.2, bf16[512,2,128,1]{0,2,3,1:T(8,128)(2,1)} %bitcast.76, bf16[256,2,8,128]{3,0,2,1:T(8,128)(2,1)} %get-tuple-element.327), kind=kOutput, calls=%fused_computation.2.clone.1 | convolution fusion | flops 543158272 | bytes 9846784 | tf_op jit(solution)/shard_map/while/body/thgd,khd->thgk/dot_general | solution.py:133
  283.5 1.9 bitcast_add_fusion.2
  287.2 1.9 constant_dynamic-slice_fusion.3
  290.1 1.8 copy.49
  291.9 3.3 %fusion.37 = (f32[256,2,8]{0,2,1:T(8,128)S(1)}, f32[2,512,256,8]{2,1,3,0:T(8,128)S(1)}) fusion(pred[256,512]{0,1:T(8,128)(4,1)S(1)} %and_and_fusion.2, bf16[512,2,128,1]{0,2,3,1:T(8,128)(2,1)} %bitcast.76, bf16[256,2,8,128]{3,0,2,1:T(8,128)(2,1)} %get-tuple-element.327), kind=kOutput, calls=%fused_computation.2.clone.1 | convolution fusion | flops 543158272 | bytes 9846784 | tf_op jit(solution)/shard_map/while/body/thgd,khd->thgk/dot_general | solution.py:133
  295.2 1.9 bitcast_add_fusion.2
  297.2 1.2 divide_convert_fusion
  298.3 2.3 copy.40
  (122 shorter events, 31.4 us)
Async XLA Ops:
  0.0 12.9 %copy-start = (bf16[2048,256]{1,0:T(8,128)(2,1)S(1)}, bf16[2048,256]{1,0:T(8,128)(2,1)}, u32[]{:S(2)}) copy-start(bf16[2048,256]{1,0:T(8,128)(2,1)} %param.14) | copy-start | bytes 3145732
  0.0 6.6 %copy-start.13 = (s32[32]{0:T(128)S(1)}, s32[32]{0:T(128)}, u32[]{:S(2)}) copy-start(s32[32]{0:T(128)} %param.17) | copy-start | bytes 388
  2.2 8.3 %copy-start.10 = (f32[2048]{0:T(1024)S(1)}, f32[2048]{0:T(1024)}, u32[]{:S(2)}) copy-start(f32[2048]{0:T(1024)} %param.11) | copy-start | bytes 24580
  2.2 6.5 %all-to-all-start = ((bf16[2,128,2048]{2,1,0:T(8,128)(2,1)}), bf16[2,128,2048]{2,1,0:T(8,128)(2,1)S(1)}, u32[]{:S(2)}, u32[]{:S(2)}) async-start(bf16[2,128,2048]{2,1,0:T(8,128)(2,1)} %broadcast_in_dim.41), calls=%async_computation | async-start | bytes 2097152 | tf_op jit(solution)/shard_map/all_to_all | solution.py:14
  10.5 1.3 copy-start.11
  10.9 1.1 copy-start.4
  11.8 0.6 copy-start.6
  11.8 0.6 copy-start.8
  13.3 9.7 %collective-permute-start.1 = (bf16[2,256,256]{2,1,0:T(8,128)(2,1)S(1)}, bf16[2,256,256]{2,1,0:T(8,128)(2,1)S(1)}, u32[]{:S(2)}, u32[]{:S(2)}) collective-permute-start(bf16[2,256,256]{2,1,0:T(8,128)(2,1)S(1)} %pad_maximum_fusion.1), channel_id=1, source_target_pairs={{0,2},{2,4},{4,6},{6,8},{8,10},{10,12},{12,14},{14,16},{16,18},{18... | collective-permute-start | bytes 786440 | tf_op jit(solution)/shard_map/ppermute | solution.py:31
  23.1 16.0 %collective-permute-start.2 = (bf16[2,512,256]{2,1,0:T(8,128)(2,1)S(1)}, bf16[2,512,256]{2,1,0:T(8,128)(2,1)S(1)}, u32[]{:S(2)}, u32[]{:S(2)}) collective-permute-start(bf16[2,512,256]{2,1,0:T(8,128)(2,1)S(1)} %maximum_maximum_fusion.1), channel_id=1, source_target_pairs={{0,4},{2,6},{4,8},{6,10},{8,12},{10,14},{12,16},{14,18},{16,20},{1... | collective-permute-start | bytes 1572872 | tf_op jit(solution)/shard_map/ppermute | solution.py:31
  39.1 37.3 %collective-permute-start.3 = (bf16[2,1024,256]{2,1,0:T(8,128)(2,1)S(1)}, bf16[2,1024,256]{2,1,0:T(8,128)(2,1)S(1)}, u32[]{:S(2)}, u32[]{:S(2)}) collective-permute-start(bf16[2,1024,256]{2,1,0:T(8,128)(2,1)S(1)} %maximum_maximum_fusion), channel_id=1, source_target_pairs={{0,8},{2,10},{4,12},{6,14},{8,16},{10,18},{12,20},{14,22},{16,24},... | collective-permute-start | bytes 3145736 | tf_op jit(solution)/shard_map/ppermute | solution.py:31
  40.4 35.3 %collective-permute-start = (bf16[2,256,256]{2,1,0:T(8,128)(2,1)S(1)}, bf16[2,256,256]{2,1,0:T(8,128)(2,1)S(1)}, u32[]{:S(2)}, u32[]{:S(2)}) collective-permute-start(bf16[2,256,256]{2,1,0:T(8,128)(2,1)S(1)} %pad_maximum_fusion.1), channel_id=1, source_target_pairs={{0,16},{2,18},{4,20},{6,22},{8,24},{10,26},{12,28},{14,30},{16,32}... | collective-permute-start | bytes 786440 | tf_op jit(solution)/shard_map/ppermute | solution.py:31
  76.5 1.0 copy-start.2
  80.7 106.8 %collective-permute-start.4 = (bf16[2,2304,256]{2,1,0:T(8,128)(2,1)}, bf16[2,2304,256]{2,1,0:T(8,128)(2,1)}, u32[]{:S(2)}, u32[]{:S(2)}) collective-permute-start(bf16[2,2304,256]{2,1,0:T(8,128)(2,1)} %constant_dynamic-update-slice_fusion), channel_id=1, source_target_pairs={{0,18},{2,20},{4,22},{6,24},{8,26},{10,28},{12,30},{14,32},{16,34}... | collective-permute-start | bytes 7077896 | tf_op jit(solution)/shard_map/ppermute | solution.py:31
  83.1 12.4 %copy-start.5 = (bf16[2,128,2048]{2,1,0:T(8,128)(2,1)S(1)}, bf16[2,128,2048]{2,1,0:T(8,128)(2,1)}, u32[]{:S(2)}) copy-start(bf16[2,128,2048]{2,1,0:T(8,128)(2,1)} %copy-done.4) | copy-start | bytes 3145732
  95.5 5.9 %copy-start.12 = (f32[128]{0:T(128)S(1)}, f32[128]{0:T(128)}, u32[]{:S(2)}) copy-start(f32[128]{0:T(128)} %param.15) | copy-start | bytes 1540
  101.3 0.8 copy-start.7
  101.4 0.9 copy-start.9
  110.3 79.1 %copy-start.3 = (bf16[2,1024,256]{2,1,0:T(8,128)(2,1)S(1)}, bf16[2,1024,256]{2,1,0:T(8,128)(2,1)}, u32[]{:S(2)}) copy-start(bf16[2,1024,256]{2,1,0:T(8,128)(2,1)} %copy-done.2) | copy-start | bytes 3145732
  189.6 2.1 copy-start.1
where the time goes:
time: 303 us; the launch traced here: 301 us
  waiting for transfers between devices  134 us (44%)
  local copies, waits for them, and re-layouts  74.7 us (25%)
  matrix products  53.7 us (18%)
  other arithmetic  25.3 us (8%)
  starting transfers between devices  10.8 us (4%)
    ppermute x5, waiting for transfers between devices, from_behind(): return lax.ppermute(x, axis, pairs)  134 us
    dot_general x9, matrix products, attend_block(): jnp.einsum('thgd,khd->thgk', query_rows, key_block, preferred_element_typ...  29.7 us
    while x18, local copies, waits for them, and re-layouts  25.9 us
    dot_general x9, matrix products, attend_block(): jnp.einsum('thgk,khd->thgd', weights.astype(jnp.bfloat16), value_block, p...  17.1 us
    slice x9, local copies, waits for them, and re-layouts, attend_block(): key_block = block_pair[0].reshape(key_span, key_heads, head_dim)  16.7 us
    dot_general x1, local copies, waits for them, and re-layouts, per_device(): jnp.dot(normalized_rows, query_weight, preferred_element_type=jnp.float32)  12.4 us
    unnamed x37, local copies, waits for them, and re-layouts  9.12 us
    and x9, other arithmetic, attend_block(): (key_doc[None, :] == query_doc[:, None]) & (key_pos[None, :] <= positions...  8.45 us
  transfers between devices with their start and end apart: 6, of which 4 were waited for; matrix products, arithmetic and copies ran while one was open for 10% of the time, Pallas kernels for 0%

commit v1 on v0

v1 whole, which is shorter than its diff:
```python
import functools
import math

import jax
import jax.numpy as jnp
from jax import lax
from jax.experimental import pallas as pl
from jax.experimental.pallas import tpu as pltpu
from jax.sharding import PartitionSpec as P


EPSILON = 1e-06
THETA = 1000000.0
RING = 4
LEVELS = 5
AXES = ("grp", "tp")


VMEM = pltpu.VMEM
SMEM = pltpu.SMEM
WHOLE = pl.BlockSpec(memory_space=VMEM)
SCALARS = pl.BlockSpec(memory_space=SMEM)
PARAMS = pltpu.CompilerParams(vmem_limit_bytes=24 * 1024 * 1024)
STACK = 2


OPPOSITE = (
    lambda up, down, ahead: (up, 0, 2, (0, -1)),
    lambda up, down, ahead: (down, 1, 2, (1, 1)),
    lambda up, down, ahead: (up, 2, 2, (2, -1)),
    lambda up, down, ahead: (down, 3, 2, (3, 1)),
    lambda up, down, ahead: (up, 4, 2, (4, -1)),
)
USES = (
    ((0, 0), (0, -1), (0, 1)),
    ((0, 2), (1, 0), (1, -1), (1, 1)),
    ((1, 2), (2, 0), (2, -1), (2, 1)),
    ((2, 2), (3, 0), (3, -1), (3, 1)),
    ((3, 2), (4, 0), (4, -1), (4, 1)),
    ((4, 2),),
)


def normed_and_rotated(head, gain, cosine, sine):
    scaled = head * lax.rsqrt(jnp.mean(head * head, axis=-1, keepdims=True) + EPSILON) * gain
    return scaled * cosine + pltpu.roll(scaled, scaled.shape[-1] // 2, 1) * sine


def normed_rows(tokens, gain):
    floated = tokens.astype(jnp.float32)
    scale = lax.rsqrt(jnp.mean(floated * floated, axis=-1, keepdims=True) + EPSILON)
    return (floated * scale * gain).astype(jnp.bfloat16)


def keys_values(normed, wk, wv, key_gain, cosine, sine):
    raw = jnp.dot(normed, wk, preferred_element_type=jnp.float32)
    value = jnp.dot(normed, wv, preferred_element_type=jnp.float32).astype(jnp.bfloat16)
    dim = key_gain.shape[1]
    key = [
        normed_and_rotated(raw[:, at : at + dim], key_gain, cosine, sine).astype(jnp.bfloat16)
        for at in range(0, raw.shape[1], dim)
    ]
    return jnp.concatenate(key, axis=1), value


def half_at(core, half):
    return pl.ds(pl.multiple_of(core * half, half), half)


def table_kernel(lengths, info, opening, cosine, sine):
    rows, dim = cosine.shape
    shard = lax.axis_index("grp") * lax.axis_size("tp") + lax.axis_index("tp")
    first_row = shard * rows
    last_row = first_row + rows - 1

    def bounds(index, carry):
        finish, lowest, highest = carry
        finish = finish + lengths[index]
        return (
            finish,
            jnp.where(finish <= first_row, finish, lowest),
            jnp.where(finish <= last_row, finish, highest),
        )

    zero = jnp.int32(0)
    count = lengths.shape[0]
    _, lowest, highest = lax.fori_loop(0, count, bounds, (zero, zero, zero))
    info[0] = shard
    info[1] = lowest
    info[2] = highest
    position = first_row + lax.broadcasted_iota(jnp.int32, opening.shape, 0)
    opening[...] = jnp.full(opening.shape, lowest, jnp.int32)

    def mark(index, finish):
        finish = finish + lengths[index]

        @pl.when((finish > first_row) & (finish <= last_row))
        def _():
            opening[...] = jnp.where(position >= finish, finish, opening[...])

        return finish

    lax.fori_loop(0, count, mark, zero)
    halfway = dim // 2
    lane = lax.broadcasted_iota(jnp.int32, (1, dim), 1)
    index = jnp.where(lane < halfway, lane, lane - halfway).astype(jnp.float32)
    inverse = jnp.exp(-(2.0 * index / dim) * math.log(THETA))
    angles = (position - opening[...]).astype(jnp.float32) * inverse
    cosine[...] = jnp.cos(angles)
    sine[...] = jnp.where(lane < halfway, -1.0, 1.0) * jnp.sin(angles)


def key_value_kernel(own, other, gain, wk, wv, key_gain, cosine, sine, normed, kv):
    half = own.shape[0]
    rows = 2 * half
    core = lax.axis_index("srv")
    normed[half_at(core, half), :] = normed_rows(own[...], gain[...])
    normed[half_at(1 - core, half), :] = normed_rows(other[...], gain[...])
    key, value = keys_values(
        normed[...], wk[...], wv[...], key_gain[...], cosine[...], sine[...]
    )
    kv[0:rows, :] = key
    kv[rows : 2 * rows, :] = value


def query_kernel(factor, tile, normed, wq, query_gain, cosine, sine, query):
    rows, dim = cosine.shape
    steps = wq.shape[1] // tile

    def raw_of(step):
        return jnp.dot(
            normed[...], wq[:, step * tile : (step + 1) * tile], preferred_element_type=jnp.float32
        )

    raw = raw_of(0)
    for step in range(steps):
        later = raw_of(step + 1) if step + 1 < steps else None
        for part in range(tile // dim):
            head = step * (tile // dim) + part
            rotated = normed_and_rotated(
                raw[:, part * dim : (part + 1) * dim], query_gain[...], cosine[...], sine[...]
            )
            query[head * rows : (head + 1) * rows, :] = (rotated * factor).astype(jnp.bfloat16)
        raw = later


def attend_kernel(places, first, last, heads, info, query, opening, *refs):
    count = len(places)
    chunks = refs[:count]
    refs = refs[count if first else count + 2 :]
    acc, den = refs[:2]
    held, bias, fars, sems = refs[-4:]
    dim = query.shape[1]
    rows = query.shape[0] // heads
    shard, lowest, highest_open = info[0], info[1], info[2]
    column = lax.rem(shard, RING)
    first_row = shard * rows
    reach = shard - lax.div(lowest, rows)

    for index, (level, offset) in enumerate(places):
        far = RING * level + column - lax.rem(column + offset + RING, RING)
        wanted = (far >= 0) & (far <= reach)
        fars[index] = jnp.where(wanted, far, -1)

        @pl.when(wanted)
        def _():
            pltpu.make_async_copy(chunks[index], held.at[index], sems.at[index]).start()

    if first:
        acc[...] = jnp.zeros_like(acc)
        den[...] = jnp.zeros_like(den)

    stack = STACK * rows
    groups = heads * dim // chunks[0].shape[1]

    def scores_of(slot, part):
        cols = pl.ds((part * STACK // groups) * dim, dim)
        return lax.dot_general(
            query[part * stack : (part + 1) * stack, :],
            held[slot, 0:rows, cols],
            (((1,), (1,)), ((), ())),
            preferred_element_type=jnp.float32,
        )

    def block(slot):
        scores = scores_of(slot, 0)
        for part in range(heads // STACK):
            later = scores_of(slot, part + 1) if (part + 1) * STACK < heads else None
            cols = pl.ds((part * STACK // groups) * dim, dim)
            weights = jnp.exp2(scores + jnp.concatenate([bias[...]] * STACK, axis=0))
            lanes = weights[:, 0:dim]
            for at in range(dim, rows, dim):
                lanes = lanes + weights[:, at : at + dim]
            den[part * stack : (part + 1) * stack, :] += lanes
            acc[part * stack : (part + 1) * stack, :] += jnp.dot(
                weights.astype(jnp.bfloat16),
                held[slot, rows : 2 * rows, cols],
                preferred_element_type=jnp.float32,
            )
            scores = later

    def step(slot, carry):
        far = fars[slot]

        @pl.when(far >= 0)
        def _():
            pltpu.make_async_copy(chunks[0], held.at[slot], sems.at[slot]).wait()
            start = (shard - far) * rows
            whole = (start >= highest_open) & (far > 0)

            @pl.when(whole)
            def _():
                bias[...] = jnp.zeros_like(bias)

            @pl.when(jnp.logical_not(whole))
            def _():
                key_at = start + lax.broadcasted_iota(jnp.int32, (rows, rows), 1)
                query_at = first_row + lax.broadcasted_iota(jnp.int32, (rows, rows), 0)
                allowed = (key_at >= opening[:, 0:1]) & (key_at <= query_at)
                bias[...] = jnp.where(allowed, 0.0, -1e30)

            block(slot)

        return carry

    lax.fori_loop(0, count, step, 0)
    if last:
        out = refs[2]
        for head in range(heads):
            part = pl.ds(head * rows, rows)
            share = 1.0 / jnp.sum(den[part, :], axis=-1, keepdims=True)
            out[:, head * dim : (head + 1) * dim] = (acc[part, :] * share).astype(jnp.bfloat16)


def attend(places, chunks, info, query, opening, carried, last, heads):
    stacked, dim = query.shape
    rows = stacked // heads
    first = carried is None
    count = len(places)
    state = jax.ShapeDtypeStruct((stacked, dim), jnp.float32)
    out_shape = (state, state)
    if last:
        out_shape += (jax.ShapeDtypeStruct((rows, heads * dim), jnp.bfloat16),)
    pairs = count * stacked * rows
    return pl.pallas_call(
        functools.partial(attend_kernel, places, first, last, heads),
        out_shape=out_shape,
        in_specs=[SCALARS, WHOLE, WHOLE]
        + [pl.BlockSpec(memory_space=pl.ANY)] * count
        + ([] if first else [WHOLE, WHOLE]),
        out_specs=(WHOLE,) * len(out_shape),
        input_output_aliases={} if first else {3 + count: 0, 4 + count: 1},
        scratch_shapes=[
            VMEM((count, 2 * rows, chunks[0].shape[1]), jnp.bfloat16),
            VMEM((rows, rows), jnp.float32),
            SMEM((count,), jnp.int32),
            pltpu.SemaphoreType.DMA((count,)),
        ],
        compiler_params=PARAMS,
        cost_estimate=pl.CostEstimate(
            flops=4 * pairs * dim, bytes_accessed=8 << 20, transcendentals=pairs
        ),
        name="attend",
    )(info, query, opening, *chunks, *([] if first else carried))


def per_device(
    tokens, norm_gain, query_weight, key_matrix, value_matrix, query_gain, key_gain, lengths
):
    half, width = tokens.shape
    rows = 2 * half
    dim = query_gain.shape[0]
    pair = key_matrix.shape[1]
    heads = query_weight.shape[1] // dim
    shards = lax.axis_size("grp") * lax.axis_size("tp")

    other = lax.ppermute(tokens, "srv", [(0, 1), (1, 0)])
    gain, key_gain, query_gain = norm_gain[None, :], key_gain[None, :], query_gain[None, :]
    table = jax.ShapeDtypeStruct((rows, dim), jnp.float32)
    normed_shape = jax.ShapeDtypeStruct((rows, width), jnp.bfloat16)
    kv_shape = jax.ShapeDtypeStruct((2 * rows, pair), jnp.bfloat16)
    info, opening, cosine, sine = pl.pallas_call(
        table_kernel,
        out_shape=(
            jax.ShapeDtypeStruct((4,), jnp.int32),
            jax.ShapeDtypeStruct((rows, dim), jnp.int32),
            table,
            table,
        ),
        in_specs=[SCALARS],
        out_specs=(SCALARS,) + (WHOLE,) * 3,
        compiler_params=PARAMS,
        cost_estimate=pl.CostEstimate(flops=4 << 30, bytes_accessed=12 << 20, transcendentals=0),
        name="tables",
    )(lengths)
    normed, kv = pl.pallas_call(
        key_value_kernel,
        out_shape=(normed_shape, kv_shape),
        in_specs=[WHOLE] * 8,
        out_specs=(WHOLE, WHOLE),
        compiler_params=PARAMS,
        cost_estimate=pl.CostEstimate(flops=2 << 30, bytes_accessed=6 << 20, transcendentals=0),
        name="keys_values",
    )(tokens, other, gain, key_matrix, value_matrix, key_gain, cosine, sine)
    query_call = pl.pallas_call(
        functools.partial(query_kernel, dim**-0.5 * math.log2(math.e), 2 * dim),
        out_shape=jax.ShapeDtypeStruct((heads * rows, dim), jnp.bfloat16),
        in_specs=[WHOLE] * 5,
        out_specs=WHOLE,
        compiler_params=PARAMS,
        cost_estimate=pl.CostEstimate(
            flops=2 * rows * width * heads * dim, bytes_accessed=11 << 20, transcendentals=0
        ),
        name="queries",
    )
    query = query_call(normed, query_weight, query_gain, cosine, sine)

    def ring(step):
        return [
            (s, s - s % RING + (s + step) % RING) for s in range(shards)
        ]

    up = functools.partial(lax.ppermute, axis_name=AXES, perm=ring(1))
    down = functools.partial(lax.ppermute, axis_name=AXES, perm=ring(-1))
    ahead = functools.partial(
        lax.ppermute, axis_name=AXES, perm=[(s, (s + RING) % shards) for s in range(shards)]
    )

    held = {(0, 0): kv}

    def bring(move, level, offset, source):
        held[level, offset] = move(held[source])

    def use(places, carried, last=False):
        return attend(places, [held[p] for p in places], info, query, opening, carried, last, heads)

    def fetch(level):
        if level:
            bring(ahead, level, 0, (level - 1, 0))
        bring(up, level, -1, (level, 0))
        bring(down, level, 1, (level, 0))

    for level in range(LEVELS):
        fetch(level)
        bring(*OPPOSITE[level](up, down, ahead))
    carried = None
    for number, places in enumerate(USES):
        carried = use(places, carried, number == len(USES) - 1)
    return carried[2]


def solution(mesh):
    placed = (
        P(("grp", "tp", "srv"), None),
        P(),
        P(None, "srv"),
        P(None, "srv"),
        P(None, "srv"),
        P(),
        P(),
        P(),
    )
    return jax.shard_map(
        per_device, mesh=mesh, in_specs=placed, out_specs=P(AXES, "srv"), check_vma=False
    )
```

time: 303 us -> 83 us (0.27)
  the two profiles are of different devices: /device:TPU:255 before, /device:TPU:254 now
where the time goes in v1:
time: 83 us; the launch traced here: 82.9 us
  Pallas kernels  39 us (47%)
  starting transfers between devices  29.7 us (36%)
  waiting for transfers between devices  13 us (16%)
    pallas_call x6, Pallas kernels, attend(): pl.pallas_call(functools.partial(attend_kernel, places, first, last, head...  33.1 us
    ppermute x19, starting transfers between devices, bring(): held[level, offset] = move(held[source])  29.6 us
    ppermute x19, waiting for transfers between devices, bring(): held[level, offset] = move(held[source])  13 us
    pallas_call x1, Pallas kernels, per_device(): query = query_call(normed, query_weight, query_gain, cosine, sine)  2.81 us
    pallas_call x1, Pallas kernels, per_device(): pl.pallas_call(table_kernel, out_shape=(jax.ShapeDtypeStruct((4,), jnp.in...  1.85 us
  transfers between devices with their start and end apart: 20, of which 4 were waited for; matrix products, arithmetic and copies ran while one was open for 0% of the time, Pallas kernels for 43%

profile of v1, /device:TPU:254, one launch (start us, length us, event | category | flops | bytes accessed | tf_op | source)
XLA Modules:
  0.0 82.9 jit_solution(7683895247597155720)
XLA Ops:
  0.0 0.0 copy-start.4
  0.0 0.0 copy-start.5
  0.0 0.0 copy-start.2
  0.0 0.0 copy-start.3
  0.0 0.1 collective-permute-start
  0.1 0.0 copy-start.6
  0.1 0.8 copy-done.6
  0.9 0.0 copy-start.7
  0.9 1.8 %tables.1 = (s32[4]{0:T(128)S(1)}, s32[256,128]{1,0:T(8,128)S(1)}, f32[256,128]{1,0:T(8,128)S(1)}, f32[256,128]{1,0:T(8,128)S(1)}) custom-call(s32[32]{0:T(128)S(1)} %copy-done.6), custom_call_target="tpu_custom_call" | custom-call | flops 4294967296 | bytes 12582912 | tf_op jit(solution)/shard_map/tables/pallas_call | solution.py:282
  2.8 0.0 collective-permute-done.other
  2.8 0.0 copy-done.4
  2.8 0.0 copy-done.5
  2.8 0.0 copy-done.2
  2.8 0.0 copy-done.3
  2.8 0.0 copy-done.7
  2.8 0.0 copy-start.1
  2.9 1.3 %keys_values.1 = (bf16[256,2048]{1,0:T(8,128)(2,1)S(1)}, bf16[512,256]{1,0:T(8,128)(2,1)S(1)}) custom-call(bf16[128,2048]{1,0:T(8,128)(2,1)S(1)} %copy-done.4, bf16[128,2048]{1,0:T(8,128)(2,1)S(1)} %collective-permute-done.other, f32[1,2048]{1,0:T(1,128)S(1)} %bitcast.4, bf16[2048,256]{1,0:T(8,128)(2,1)S(1)} %copy-done.2, bf16[2048,256]{1,0:T(8,128)(2,1)S(1)} %copy-done.3, ...), custom_call_target="tpu_custom_call" | custom-call | flops 2147483648 | bytes 6291456 | tf_op jit(solution)/shard_map/keys_values/pallas_call | solution.py:296
  4.1 0.1 collective-permute-start.1
  4.2 8.6 %collective-permute-done.1.refs_1_ = bf16[512,256]{1,0:T(8,128)(2,1)S(1)} collective-permute-done((bf16[512,256]{1,0:T(8,128)(2,1)S(1)}, bf16[512,256]{1,0:T(8,128)(2,1)S(1)}, u32[]{:S(2)}, u32[]{:S(2)}) %collective-permute-start.1) | collective-permute-done | bytes 262176 | tf_op jit(solution)/shard_map/ppermute | solution.py:332
  12.8 3.6 %collective-permute-start.2 = (bf16[512,256]{1,0:T(8,128)(2,1)S(1)}, bf16[512,256]{1,0:T(8,128)(2,1)S(1)}, u32[]{:S(2)}, u32[]{:S(2)}) collective-permute-start(bf16[512,256]{1,0:T(8,128)(2,1)S(1)} %collective-permute-done.1.refs_1_), channel_id=1, source_target_pairs={{0,8},{2,10},{4,12},{6,14},{8,16},{10,18},{12,20},{14,22},{16,24},... | collective-permute-start | bytes 786440 | tf_op jit(solution)/shard_map/ppermute | solution.py:332
  16.4 0.2 collective-permute-start.16
  16.6 1.8 %collective-permute-start.19 = (bf16[512,256]{1,0:T(8,128)(2,1)S(1)}, bf16[512,256]{1,0:T(8,128)(2,1)S(1)}, u32[]{:S(2)}, u32[]{:S(2)}) collective-permute-start(bf16[512,256]{1,0:T(8,128)(2,1)S(1)} %get-tuple-element.27.refs_0_), channel_id=1, source_target_pairs={{0,6},{2,0},{4,2},{6,4},{8,14},{10,8},{12,10},{14,12},{16,22},{18,... | collective-permute-start | bytes 786440 | tf_op jit(solution)/shard_map/ppermute | solution.py:332
  18.4 0.7 collective-permute-start.13
  19.2 2.8 %collective-permute-done.2.refs_1_ = bf16[512,256]{1,0:T(8,128)(2,1)S(1)} collective-permute-done((bf16[512,256]{1,0:T(8,128)(2,1)S(1)}, bf16[512,256]{1,0:T(8,128)(2,1)S(1)}, u32[]{:S(2)}, u32[]{:S(2)}) %collective-permute-start.2) | collective-permute-done | bytes 262176 | tf_op jit(solution)/shard_map/ppermute | solution.py:332
  22.0 5.8 %collective-permute-start.3 = (bf16[512,256]{1,0:T(8,128)(2,1)S(1)}, bf16[512,256]{1,0:T(8,128)(2,1)S(1)}, u32[]{:S(2)}, u32[]{:S(2)}) collective-permute-start(bf16[512,256]{1,0:T(8,128)(2,1)S(1)} %collective-permute-done.2.refs_1_), channel_id=1, source_target_pairs={{0,8},{2,10},{4,12},{6,14},{8,16},{10,18},{12,20},{14,22},{16,24},... | collective-permute-start | bytes 786440 | tf_op jit(solution)/shard_map/ppermute | solution.py:332
  27.8 0.2 collective-permute-start.18
  27.9 0.0 collective-permute-done.16.refs_1_
  27.9 1.6 %collective-permute-start.17 = (bf16[512,256]{1,0:T(8,128)(2,1)S(1)}, bf16[512,256]{1,0:T(8,128)(2,1)S(1)}, u32[]{:S(2)}, u32[]{:S(2)}) collective-permute-start(bf16[512,256]{1,0:T(8,128)(2,1)S(1)} %collective-permute-done.16.refs_1_), channel_id=1, source_target_pairs={{0,2},{2,4},{4,6},{6,0},{8,10},{10,12},{12,14},{14,8},{16,18},{18,... | collective-permute-start | bytes 786440 | tf_op jit(solution)/shard_map/ppermute | solution.py:332
  29.5 0.0 collective-permute-done.19.refs_2_
  29.5 1.6 %collective-permute-start.10 = (bf16[512,256]{1,0:T(8,128)(2,1)S(1)}, bf16[512,256]{1,0:T(8,128)(2,1)S(1)}, u32[]{:S(2)}, u32[]{:S(2)}) collective-permute-start(bf16[512,256]{1,0:T(8,128)(2,1)S(1)} %collective-permute-done.2.refs_1_), channel_id=1, source_target_pairs={{0,2},{2,4},{4,6},{6,0},{8,10},{10,12},{12,14},{14,8},{16,18},{18,... | collective-permute-start | bytes 786440 | tf_op jit(solution)/shard_map/ppermute | solution.py:332
  31.1 0.0 collective-permute-done.13.refs_3_
  31.1 0.4 collective-permute-start.15
  31.6 0.9 %collective-permute-done.3.refs_1_ = bf16[512,256]{1,0:T(8,128)(2,1)S(1)} collective-permute-done((bf16[512,256]{1,0:T(8,128)(2,1)S(1)}, bf16[512,256]{1,0:T(8,128)(2,1)S(1)}, u32[]{:S(2)}, u32[]{:S(2)}) %collective-permute-start.3) | collective-permute-done | bytes 262176 | tf_op jit(solution)/shard_map/ppermute | solution.py:332
  32.4 5.8 %collective-permute-start.4 = (bf16[512,256]{1,0:T(8,128)(2,1)S(1)}, bf16[512,256]{1,0:T(8,128)(2,1)S(1)}, u32[]{:S(2)}, u32[]{:S(2)}) collective-permute-start(bf16[512,256]{1,0:T(8,128)(2,1)S(1)} %collective-permute-done.3.refs_1_), channel_id=1, source_target_pairs={{0,8},{2,10},{4,12},{6,14},{8,16},{10,18},{12,20},{14,22},{16,24},... | collective-permute-start | bytes 786440 | tf_op jit(solution)/shard_map/ppermute | solution.py:332
  38.2 0.0 copy-done
  38.3 0.0 copy-done.1
  38.3 2.8 %queries.1.query = bf16[4096,128]{1,0:T(8,128)(2,1)S(1)} custom-call(bf16[256,2048]{1,0:T(8,128)(2,1)S(1)} %get-tuple-element.25.normed, bf16[2048,2048]{1,0:T(8,128)(2,1)S(1)} %copy-done, f32[1,128]{1,0:T(1,128)S(1)} %bitcast.3, f32[256,128]{1,0:T(8,128)S(1)} %get-tuple-element.23.cosine, f32[256,128]{1,0:T(8,128)S(1)} %get-tuple-element.24.sine), custom_call_target="tpu_custom_call" | custom-call | flops 2147483648 | bytes 11534336 | tf_op jit(solution)/shard_map/queries/pallas_call | solution.py:316
  41.1 0.0 collective-permute-done.18.refs_2_
  41.1 0.8 collective-permute-start.14
  41.9 0.7 collective-permute-done.17.refs_0_
  42.6 0.7 collective-permute-start.7
  43.3 5.7 %attend.6 = (f32[4096,128]{1,0:T(8,128)S(1)}, f32[4096,128]{1,0:T(8,128)S(1)}) custom-call(s32[4]{0:T(128)S(1)} %get-tuple-element.22.info, bf16[4096,128]{1,0:T(8,128)(2,1)S(1)} %queries.1.query, s32[256,128]{1,0:T(8,128)S(1)} %get-tuple-element.26.opening, bf16[512,256]{1,0:T(8,128)(2,1)S(1)} %get-tuple-element.27.refs_0_, ...), custom_call_target="tpu_custom_call" | custom-call | flops 1610612736 | bytes 8388608 | tf_op jit(solution)/shard_map/attend/pallas_call | solution.py:245
  49.0 0.0 collective-permute-done.10.refs_2_
  49.0 0.1 collective-permute-start.12
  49.1 0.0 collective-permute-done.15.refs_3_
  49.1 1.4 %collective-permute-start.11 = (bf16[512,256]{1,0:T(8,128)(2,1)S(1)}, bf16[512,256]{1,0:T(8,128)(2,1)S(1)}, u32[]{:S(2)}, u32[]{:S(2)}) collective-permute-start(bf16[512,256]{1,0:T(8,128)(2,1)S(1)} %collective-permute-done.10.refs_2_), channel_id=1, source_target_pairs={{0,2},{2,4},{4,6},{6,0},{8,10},{10,12},{12,14},{14,8},{16,18},{18,... | collective-permute-start | bytes 786440 | tf_op jit(solution)/shard_map/ppermute | solution.py:332
  50.5 0.0 collective-permute-done.4.refs_1_
  50.5 0.1 collective-permute-start.5
  50.6 7.0 %attend.7 = (f32[4096,128]{1,0:T(8,128)S(1)}, f32[4096,128]{1,0:T(8,128)S(1)}) custom-call(s32[4]{0:T(128)S(1)} %get-tuple-element.22.info, bf16[4096,128]{1,0:T(8,128)(2,1)S(1)} %queries.1.query, s32[256,128]{1,0:T(8,128)S(1)} %get-tuple-element.26.opening, ...), custom_call_target="tpu_custom_call", output_to_operand_aliasing={{0}: (7, {}), {1}: (8, {})} | custom-call | flops 2147483648 | bytes 8388608 | tf_op jit(solution)/shard_map/attend/pallas_call | solution.py:245
  57.7 0.0 collective-permute-done.14.refs_0_
  57.7 1.7 %collective-permute-start.9 = (bf16[512,256]{1,0:T(8,128)(2,1)S(1)}, bf16[512,256]{1,0:T(8,128)(2,1)S(1)}, u32[]{:S(2)}, u32[]{:S(2)}) collective-permute-start(bf16[512,256]{1,0:T(8,128)(2,1)S(1)} %collective-permute-done.4.refs_1_), channel_id=1, source_target_pairs={{0,6},{2,0},{4,2},{6,4},{8,14},{10,8},{12,10},{14,12},{16,22},{18,... | collective-permute-start | bytes 786440 | tf_op jit(solution)/shard_map/ppermute | solution.py:332
  59.4 0.0 collective-permute-done.7.refs_3_
  59.4 0.1 collective-permute-start.8
  59.5 7.3 %attend.8 = (f32[4096,128]{1,0:T(8,128)S(1)}, f32[4096,128]{1,0:T(8,128)S(1)}) custom-call(s32[4]{0:T(128)S(1)} %get-tuple-element.22.info, bf16[4096,128]{1,0:T(8,128)(2,1)S(1)} %queries.1.query, s32[256,128]{1,0:T(8,128)S(1)} %get-tuple-element.26.opening, ...), custom_call_target="tpu_custom_call", output_to_operand_aliasing={{0}: (7, {}), {1}: (8, {})} | custom-call | flops 2147483648 | bytes 8388608 | tf_op jit(solution)/shard_map/attend/pallas_call | solution.py:245
  66.7 0.0 collective-permute-done.5.refs_2_
  66.7 2.9 %collective-permute-start.6 = (bf16[512,256]{1,0:T(8,128)(2,1)S(1)}, bf16[512,256]{1,0:T(8,128)(2,1)S(1)}, u32[]{:S(2)}, u32[]{:S(2)}) collective-permute-start(bf16[512,256]{1,0:T(8,128)(2,1)S(1)} %collective-permute-done.5.refs_2_), channel_id=1, source_target_pairs={{0,2},{2,4},{4,6},{6,0},{8,10},{10,12},{12,14},{14,8},{16,18},{18,... | collective-permute-start | bytes 786440 | tf_op jit(solution)/shard_map/ppermute | solution.py:332
  69.6 0.0 collective-permute-done.12.refs_2_
  69.6 0.0 collective-permute-done.11.refs_0_
  69.6 7.0 %attend.9 = (f32[4096,128]{1,0:T(8,128)S(1)}, f32[4096,128]{1,0:T(8,128)S(1)}) custom-call(s32[4]{0:T(128)S(1)} %get-tuple-element.22.info, bf16[4096,128]{1,0:T(8,128)(2,1)S(1)} %queries.1.query, s32[256,128]{1,0:T(8,128)S(1)} %get-tuple-element.26.opening, ...), custom_call_target="tpu_custom_call", output_to_operand_aliasing={{0}: (7, {}), {1}: (8, {})} | custom-call | flops 2147483648 | bytes 8388608 | tf_op jit(solution)/shard_map/attend/pallas_call | solution.py:245
  76.7 0.0 collective-permute-done.9.refs_3_
  76.7 0.0 collective-permute-done.8.refs_0_
  76.7 3.9 %attend.10 = (f32[4096,128]{1,0:T(8,128)S(1)}, f32[4096,128]{1,0:T(8,128)S(1)}) custom-call(s32[4]{0:T(128)S(1)} %get-tuple-element.22.info, bf16[4096,128]{1,0:T(8,128)(2,1)S(1)} %queries.1.query, s32[256,128]{1,0:T(8,128)S(1)} %get-tuple-element.26.opening, ...), custom_call_target="tpu_custom_call", output_to_operand_aliasing={{0}: (7, {}), {1}: (8, {})} | custom-call | flops 2147483648 | bytes 8388608 | tf_op jit(solution)/shard_map/attend/pallas_call | solution.py:245
  80.6 0.0 collective-permute-done.6.refs_0_
  80.6 2.2 %attend.11 = (f32[4096,128]{1,0:T(8,128)S(1)}, f32[4096,128]{1,0:T(8,128)S(1)}, bf16[256,2048]{1,0:T(8,128)(2,1)}) custom-call(s32[4]{0:T(128)S(1)} %get-tuple-element.22.info, bf16[4096,128]{1,0:T(8,128)(2,1)S(1)} %queries.1.query, s32[256,128]{1,0:T(8,128)S(1)} %get-tuple-element.26.opening, ...), custom_call_target="tpu_custom_call", output_to_operand_aliasing={{0}: (4, {}), {1}: (5, {})} | custom-call | flops 536870912 | bytes 8388608 | tf_op jit(solution)/shard_map/attend/pallas_call | solution.py:245
  (1 shorter events, 0.0 us)
Async XLA Ops:
  0.0 2.8 %copy-start.4 = (bf16[128,2048]{1,0:T(8,128)(2,1)S(1)}, bf16[128,2048]{1,0:T(8,128)(2,1)}, u32[]{:S(2)}) copy-start(bf16[128,2048]{1,0:T(8,128)(2,1)} %own.1) | copy-start | bytes 1572868
  0.0 2.8 %copy-start.5 = (f32[2048]{0:T(1024)S(1)}, f32[2048]{0:T(1024)}, u32[]{:S(2)}) copy-start(f32[2048]{0:T(1024)} %param.9) | copy-start | bytes 24580
  0.0 2.8 %copy-start.2 = (bf16[2048,256]{1,0:T(8,128)(2,1)S(1)}, bf16[2048,256]{1,0:T(8,128)(2,1)}, u32[]{:S(2)}) copy-start(bf16[2048,256]{1,0:T(8,128)(2,1)} %wk.1) | copy-start | bytes 3145732
  0.0 2.8 %copy-start.3 = (bf16[2048,256]{1,0:T(8,128)(2,1)S(1)}, bf16[2048,256]{1,0:T(8,128)(2,1)}, u32[]{:S(2)}) copy-start(bf16[2048,256]{1,0:T(8,128)(2,1)} %wv.1) | copy-start | bytes 3145732
  0.0 2.8 %collective-permute-start = (bf16[128,2048]{1,0:T(8,128)(2,1)}, bf16[128,2048]{1,0:T(8,128)(2,1)S(1)}, u32[]{:S(2)}, u32[]{:S(2)}) collective-permute-start(bf16[128,2048]{1,0:T(8,128)(2,1)} %own.1), channel_id=1, source_target_pairs={{0,1},{1,0},{2,3},{3,2},{4,5},{5,4},{6,7},{7,6},{8,9},{9,8},{10,11... | collective-permute-start | bytes 1572872 | tf_op jit(solution)/shard_map/ppermute | solution.py:277
  0.1 0.8 copy-start.6
  0.9 1.9 %copy-start.7 = (f32[128]{0:T(128)S(1)}, f32[128]{0:T(128)}, u32[]{:S(2)}) copy-start(f32[128]{0:T(128)} %param.14) | copy-start | bytes 1540
  0.9 37.3 %copy-start = (bf16[2048,2048]{1,0:T(8,128)(2,1)S(1)}, bf16[2048,2048]{1,0:T(8,128)(2,1)}, u32[]{:S(2)}) copy-start(bf16[2048,2048]{1,0:T(8,128)(2,1)} %wq.1) | copy-start | bytes 25165828
  2.8 35.4 %copy-start.1 = (f32[128]{0:T(128)S(1)}, f32[128]{0:T(128)}, u32[]{:S(2)}) copy-start(f32[128]{0:T(128)} %param.13) | copy-start | bytes 1540
  4.1 8.7 %collective-permute-start.1 = (bf16[512,256]{1,0:T(8,128)(2,1)S(1)}, bf16[512,256]{1,0:T(8,128)(2,1)S(1)}, u32[]{:S(2)}, u32[]{:S(2)}) collective-permute-start(bf16[512,256]{1,0:T(8,128)(2,1)S(1)} %get-tuple-element.27.refs_0_), channel_id=1, source_target_pairs={{0,8},{2,10},{4,12},{6,14},{8,16},{10,18},{12,20},{14,22},{16,24},... | collective-permute-start | bytes 786440 | tf_op jit(solution)/shard_map/ppermute | solution.py:332
  12.8 9.1 %collective-permute-start.2 = (bf16[512,256]{1,0:T(8,128)(2,1)S(1)}, bf16[512,256]{1,0:T(8,128)(2,1)S(1)}, u32[]{:S(2)}, u32[]{:S(2)}) collective-permute-start(bf16[512,256]{1,0:T(8,128)(2,1)S(1)} %collective-permute-done.1.refs_1_), channel_id=1, source_target_pairs={{0,8},{2,10},{4,12},{6,14},{8,16},{10,18},{12,20},{14,22},{16,24},... | collective-permute-start | bytes 786440 | tf_op jit(solution)/shard_map/ppermute | solution.py:332
  16.4 11.5 %collective-permute-start.16 = (bf16[512,256]{1,0:T(8,128)(2,1)S(1)}, bf16[512,256]{1,0:T(8,128)(2,1)S(1)}, u32[]{:S(2)}, u32[]{:S(2)}) collective-permute-start(bf16[512,256]{1,0:T(8,128)(2,1)S(1)} %get-tuple-element.27.refs_0_), channel_id=1, source_target_pairs={{0,2},{2,4},{4,6},{6,0},{8,10},{10,12},{12,14},{14,8},{16,18},{18,... | collective-permute-start | bytes 786440 | tf_op jit(solution)/shard_map/ppermute | solution.py:332
  16.6 12.9 %collective-permute-start.19 = (bf16[512,256]{1,0:T(8,128)(2,1)S(1)}, bf16[512,256]{1,0:T(8,128)(2,1)S(1)}, u32[]{:S(2)}, u32[]{:S(2)}) collective-permute-start(bf16[512,256]{1,0:T(8,128)(2,1)S(1)} %get-tuple-element.27.refs_0_), channel_id=1, source_target_pairs={{0,6},{2,0},{4,2},{6,4},{8,14},{10,8},{12,10},{14,12},{16,22},{18,... | collective-permute-start | bytes 786440 | tf_op jit(solution)/shard_map/ppermute | solution.py:332
  18.4 12.7 %collective-permute-start.13 = (bf16[512,256]{1,0:T(8,128)(2,1)S(1)}, bf16[512,256]{1,0:T(8,128)(2,1)S(1)}, u32[]{:S(2)}, u32[]{:S(2)}) collective-permute-start(bf16[512,256]{1,0:T(8,128)(2,1)S(1)} %collective-permute-done.1.refs_1_), channel_id=1, source_target_pairs={{0,6},{2,0},{4,2},{6,4},{8,14},{10,8},{12,10},{14,12},{16,22},{18,... | collective-permute-start | bytes 786440 | tf_op jit(solution)/shard_map/ppermute | solution.py:332
  22.0 10.5 %collective-permute-start.3 = (bf16[512,256]{1,0:T(8,128)(2,1)S(1)}, bf16[512,256]{1,0:T(8,128)(2,1)S(1)}, u32[]{:S(2)}, u32[]{:S(2)}) collective-permute-start(bf16[512,256]{1,0:T(8,128)(2,1)S(1)} %collective-permute-done.2.refs_1_), channel_id=1, source_target_pairs={{0,8},{2,10},{4,12},{6,14},{8,16},{10,18},{12,20},{14,22},{16,24},... | collective-permute-start | bytes 786440 | tf_op jit(solution)/shard_map/ppermute | solution.py:332
  27.8 13.3 %collective-permute-start.18 = (bf16[512,256]{1,0:T(8,128)(2,1)S(1)}, bf16[512,256]{1,0:T(8,128)(2,1)S(1)}, u32[]{:S(2)}, u32[]{:S(2)}) collective-permute-start(bf16[512,256]{1,0:T(8,128)(2,1)S(1)} %collective-permute-done.1.refs_1_), channel_id=1, source_target_pairs={{0,2},{2,4},{4,6},{6,0},{8,10},{10,12},{12,14},{14,8},{16,18},{18,... | collective-permute-start | bytes 786440 | tf_op jit(solution)/shard_map/ppermute | solution.py:332
  27.9 14.6 %collective-permute-start.17 = (bf16[512,256]{1,0:T(8,128)(2,1)S(1)}, bf16[512,256]{1,0:T(8,128)(2,1)S(1)}, u32[]{:S(2)}, u32[]{:S(2)}) collective-permute-start(bf16[512,256]{1,0:T(8,128)(2,1)S(1)} %collective-permute-done.16.refs_1_), channel_id=1, source_target_pairs={{0,2},{2,4},{4,6},{6,0},{8,10},{10,12},{12,14},{14,8},{16,18},{18,... | collective-permute-start | bytes 786440 | tf_op jit(solution)/shard_map/ppermute | solution.py:332
  29.5 19.4 %collective-permute-start.10 = (bf16[512,256]{1,0:T(8,128)(2,1)S(1)}, bf16[512,256]{1,0:T(8,128)(2,1)S(1)}, u32[]{:S(2)}, u32[]{:S(2)}) collective-permute-start(bf16[512,256]{1,0:T(8,128)(2,1)S(1)} %collective-permute-done.2.refs_1_), channel_id=1, source_target_pairs={{0,2},{2,4},{4,6},{6,0},{8,10},{10,12},{12,14},{14,8},{16,18},{18,... | collective-permute-start | bytes 786440 | tf_op jit(solution)/shard_map/ppermute | solution.py:332
  31.1 18.0 %collective-permute-start.15 = (bf16[512,256]{1,0:T(8,128)(2,1)S(1)}, bf16[512,256]{1,0:T(8,128)(2,1)S(1)}, u32[]{:S(2)}, u32[]{:S(2)}) collective-permute-start(bf16[512,256]{1,0:T(8,128)(2,1)S(1)} %collective-permute-done.2.refs_1_), channel_id=1, source_target_pairs={{0,6},{2,0},{4,2},{6,4},{8,14},{10,8},{12,10},{14,12},{16,22},{18,... | collective-permute-start | bytes 786440 | tf_op jit(solution)/shard_map/ppermute | solution.py:332
  32.4 18.1 %collective-permute-start.4 = (bf16[512,256]{1,0:T(8,128)(2,1)S(1)}, bf16[512,256]{1,0:T(8,128)(2,1)S(1)}, u32[]{:S(2)}, u32[]{:S(2)}) collective-permute-start(bf16[512,256]{1,0:T(8,128)(2,1)S(1)} %collective-permute-done.3.refs_1_), channel_id=1, source_target_pairs={{0,8},{2,10},{4,12},{6,14},{8,16},{10,18},{12,20},{14,22},{16,24},... | collective-permute-start | bytes 786440 | tf_op jit(solution)/shard_map/ppermute | solution.py:332
  41.1 16.6 %collective-permute-start.14 = (bf16[512,256]{1,0:T(8,128)(2,1)S(1)}, bf16[512,256]{1,0:T(8,128)(2,1)S(1)}, u32[]{:S(2)}, u32[]{:S(2)}) collective-permute-start(bf16[512,256]{1,0:T(8,128)(2,1)S(1)} %collective-permute-done.13.refs_3_), channel_id=1, source_target_pairs={{0,6},{2,0},{4,2},{6,4},{8,14},{10,8},{12,10},{14,12},{16,22},{18,... | collective-permute-start | bytes 786440 | tf_op jit(solution)/shard_map/ppermute | solution.py:332
  42.6 16.8 %collective-permute-start.7 = (bf16[512,256]{1,0:T(8,128)(2,1)S(1)}, bf16[512,256]{1,0:T(8,128)(2,1)S(1)}, u32[]{:S(2)}, u32[]{:S(2)}) collective-permute-start(bf16[512,256]{1,0:T(8,128)(2,1)S(1)} %collective-permute-done.3.refs_1_), channel_id=1, source_target_pairs={{0,6},{2,0},{4,2},{6,4},{8,14},{10,8},{12,10},{14,12},{16,22},{18,... | collective-permute-start | bytes 786440 | tf_op jit(solution)/shard_map/ppermute | solution.py:332
  49.0 20.6 %collective-permute-start.12 = (bf16[512,256]{1,0:T(8,128)(2,1)S(1)}, bf16[512,256]{1,0:T(8,128)(2,1)S(1)}, u32[]{:S(2)}, u32[]{:S(2)}) collective-permute-start(bf16[512,256]{1,0:T(8,128)(2,1)S(1)} %collective-permute-done.3.refs_1_), channel_id=1, source_target_pairs={{0,2},{2,4},{4,6},{6,0},{8,10},{10,12},{12,14},{14,8},{16,18},{18,... | collective-permute-start | bytes 786440 | tf_op jit(solution)/shard_map/ppermute | solution.py:332
  49.1 20.5 %collective-permute-start.11 = (bf16[512,256]{1,0:T(8,128)(2,1)S(1)}, bf16[512,256]{1,0:T(8,128)(2,1)S(1)}, u32[]{:S(2)}, u32[]{:S(2)}) collective-permute-start(bf16[512,256]{1,0:T(8,128)(2,1)S(1)} %collective-permute-done.10.refs_2_), channel_id=1, source_target_pairs={{0,2},{2,4},{4,6},{6,0},{8,10},{10,12},{12,14},{14,8},{16,18},{18,... | collective-permute-start | bytes 786440 | tf_op jit(solution)/shard_map/ppermute | solution.py:332
  50.5 16.2 %collective-permute-start.5 = (bf16[512,256]{1,0:T(8,128)(2,1)S(1)}, bf16[512,256]{1,0:T(8,128)(2,1)S(1)}, u32[]{:S(2)}, u32[]{:S(2)}) collective-permute-start(bf16[512,256]{1,0:T(8,128)(2,1)S(1)} %collective-permute-done.4.refs_1_), channel_id=1, source_target_pairs={{0,2},{2,4},{4,6},{6,0},{8,10},{10,12},{12,14},{14,8},{16,18},{18,... | collective-permute-start | bytes 786440 | tf_op jit(solution)/shard_map/ppermute | solution.py:332
  57.7 19.0 %collective-permute-start.9 = (bf16[512,256]{1,0:T(8,128)(2,1)S(1)}, bf16[512,256]{1,0:T(8,128)(2,1)S(1)}, u32[]{:S(2)}, u32[]{:S(2)}) collective-permute-start(bf16[512,256]{1,0:T(8,128)(2,1)S(1)} %collective-permute-done.4.refs_1_), channel_id=1, source_target_pairs={{0,6},{2,0},{4,2},{6,4},{8,14},{10,8},{12,10},{14,12},{16,22},{18,... | collective-permute-start | bytes 786440 | tf_op jit(solution)/shard_map/ppermute | solution.py:332
  59.4 17.3 %collective-permute-start.8 = (bf16[512,256]{1,0:T(8,128)(2,1)S(1)}, bf16[512,256]{1,0:T(8,128)(2,1)S(1)}, u32[]{:S(2)}, u32[]{:S(2)}) collective-permute-start(bf16[512,256]{1,0:T(8,128)(2,1)S(1)} %collective-permute-done.7.refs_3_), channel_id=1, source_target_pairs={{0,6},{2,0},{4,2},{6,4},{8,14},{10,8},{12,10},{14,12},{16,22},{18,... | collective-permute-start | bytes 786440 | tf_op jit(solution)/shard_map/ppermute | solution.py:332
  66.7 13.8 %collective-permute-start.6 = (bf16[512,256]{1,0:T(8,128)(2,1)S(1)}, bf16[512,256]{1,0:T(8,128)(2,1)S(1)}, u32[]{:S(2)}, u32[]{:S(2)}) collective-permute-start(bf16[512,256]{1,0:T(8,128)(2,1)S(1)} %collective-permute-done.5.refs_2_), channel_id=1, source_target_pairs={{0,2},{2,4},{4,6},{6,0},{8,10},{10,12},{12,14},{14,8},{16,18},{18,... | collective-permute-start | bytes 786440 | tf_op jit(solution)/shard_map/ppermute | solution.py:332

commit v2 on v1

--- a/solution.py
+++ b/solution.py
@@ -12,7 +12,6 @@
 EPSILON = 1e-06
 THETA = 1000000.0
 RING = 4
-LEVELS = 5
 AXES = ("grp", "tp")
 
 
@@ -24,19 +23,40 @@
 STACK = 2
 
 
-OPPOSITE = (
-    lambda up, down, ahead: (up, 0, 2, (0, -1)),
-    lambda up, down, ahead: (down, 1, 2, (1, 1)),
-    lambda up, down, ahead: (up, 2, 2, (2, -1)),
-    lambda up, down, ahead: (down, 3, 2, (3, 1)),
-    lambda up, down, ahead: (up, 4, 2, (4, -1)),
+MOVES = (
+    (
+        ("ahead", ((0, 0),), ((1, 0),)),
+        ("up", ((0, 0),), ((0, -1),)),
+        ("down", ((0, 0),), ((0, 1),)),
+    ),
+    (
+        ("ahead", ((1, 0),), ((2, 0),)),
+        ("down", ((1, 0),), ((1, 1),)),
+        ("up", ((0, -1), (1, 0)), ((0, 2), (1, -1))),
+    ),
+    (
+        ("ahead", ((2, 0),), ((3, 0),)),
+        ("up", ((2, 0),), ((2, -1),)),
+        ("down", ((1, 1), (2, 0)), ((1, 2), (2, 1))),
+    ),
+    (
+        ("ahead", ((3, 0),), ((4, 0),)),
+        ("down", ((3, 0),), ((3, 1),)),
+        ("up", ((2, -1), (3, 0)), ((2, 2), (3, -1))),
+    ),
+    (
+        ("up", ((4, 0),), ((4, -1),)),
+        ("down", ((3, 1), (4, 0)), ((3, 2), (4, 1))),
+    ),
+    (("up", ((4, -1),), ((4, 2),)),),
 )
 USES = (
-    ((0, 0), (0, -1), (0, 1)),
-    ((0, 2), (1, 0), (1, -1), (1, 1)),
-    ((1, 2), (2, 0), (2, -1), (2, 1)),
-    ((2, 2), (3, 0), (3, -1), (3, 1)),
-    ((3, 2), (4, 0), (4, -1), (4, 1)),
+    ((0, 0),),
+    ((0, -1), (0, 1), (1, 0)),
+    ((0, 2), (1, -1), (1, 1), (2, 0)),
+    ((1, 2), (2, -1), (2, 1), (3, 0)),
+    ((2, 2), (3, -1), (3, 1), (4, 0)),
+    ((3, 2), (4, -1), (4, 1)),
     ((4, 2),),
 )
 
@@ -144,7 +164,7 @@
         raw = later
 
 
-def attend_kernel(places, first, last, heads, info, query, opening, *refs):
+def attend_kernel(places, starts, first, last, heads, info, query, opening, *refs):
     count = len(places)
     chunks = refs[:count]
     refs = refs[count if first else count + 2 :]
@@ -164,7 +184,8 @@
 
         @pl.when(wanted)
         def _():
-            pltpu.make_async_copy(chunks[index], held.at[index], sems.at[index]).start()
+            block = chunks[index].at[pl.ds(starts[index], 2 * rows), :]
+            pltpu.make_async_copy(block, held.at[index], sems.at[index]).start()
 
     if first:
         acc[...] = jnp.zeros_like(acc)
@@ -204,7 +225,7 @@
 
         @pl.when(far >= 0)
         def _():
-            pltpu.make_async_copy(chunks[0], held.at[slot], sems.at[slot]).wait()
+            pltpu.make_async_copy(held.at[slot], held.at[slot], sems.at[slot]).wait()
             start = (shard - far) * rows
             whole = (start >= highest_open) & (far > 0)
 
@@ -232,18 +253,20 @@
             out[:, head * dim : (head + 1) * dim] = (acc[part, :] * share).astype(jnp.bfloat16)
 
 
-def attend(places, chunks, info, query, opening, carried, last, heads):
+def attend(places, blocks, size, info, query, opening, carried, last, heads):
     stacked, dim = query.shape
     rows = stacked // heads
     first = carried is None
     count = len(places)
+    chunks = [chunk for chunk, _ in blocks]
+    starts = [start for _, start in blocks]
     state = jax.ShapeDtypeStruct((stacked, dim), jnp.float32)
     out_shape = (state, state)
     if last:
         out_shape += (jax.ShapeDtypeStruct((rows, heads * dim), jnp.bfloat16),)
     pairs = count * stacked * rows
     return pl.pallas_call(
-        functools.partial(attend_kernel, places, first, last, heads),
+        functools.partial(attend_kernel, places, starts, first, last, heads),
         out_shape=out_shape,
         in_specs=[SCALARS, WHOLE, WHOLE]
         + [pl.BlockSpec(memory_space=pl.ANY)] * count
@@ -251,7 +274,7 @@
         out_specs=(WHOLE,) * len(out_shape),
         input_output_aliases={} if first else {3 + count: 0, 4 + count: 1},
         scratch_shapes=[
-            VMEM((count, 2 * rows, chunks[0].shape[1]), jnp.bfloat16),
+            VMEM((count, size, chunks[0].shape[1]), jnp.bfloat16),
             VMEM((rows, rows), jnp.float32),
             SMEM((count,), jnp.int32),
             pltpu.SemaphoreType.DMA((count,)),
@@ -326,23 +349,21 @@
         lax.ppermute, axis_name=AXES, perm=[(s, (s + RING) % shards) for s in range(shards)]
     )
 
-    held = {(0, 0): kv}
-
-    def bring(move, level, offset, source):
-        held[level, offset] = move(held[source])
-
-    def use(places, carried, last=False):
-        return attend(places, [held[p] for p in places], info, query, opening, carried, last, heads)
-
-    def fetch(level):
-        if level:
-            bring(ahead, level, 0, (level - 1, 0))
-        bring(up, level, -1, (level, 0))
-        bring(down, level, 1, (level, 0))
-
-    for level in range(LEVELS):
-        fetch(level)
-        bring(*OPPOSITE[level](up, down, ahead))
+    ways = {"up": up, "down": down, "ahead": ahead}
+    held = {(0, 0): (kv, 0)}
+    size = kv.shape[0]
+    for moves in MOVES:
+        for way, sources, places in moves:
+            blocks = [held[p][0] for p in sources]
+            sent = blocks[0] if len(blocks) == 1 else jnp.concatenate(blocks, axis=0)
+            came = ways[way](sent)
+            for index, place in enumerate(places):
+                held[place] = (came, index * size)
+
+    def use(places, carried, last):
+        blocks = [held[p] for p in places]
+        return attend(places, blocks, size, info, query, opening, carried, last, heads)
+
     carried = None
     for number, places in enumerate(USES):
         carried = use(places, carried, number == len(USES) - 1)

time: 83 us -> 81.5 us (0.982)
  the two profiles are of different devices: /device:TPU:254 before, /device:TPU:246 now
where the time goes in v2:
time: 81.5 us; the launch traced here: 81.4 us
  Pallas kernels  36.7 us (45%)
  starting transfers between devices  28.2 us (35%)
  waiting for transfers between devices  15.1 us (19%)
  local copies, waits for them, and re-layouts  0.83 us (1%)
    pallas_call x7, Pallas kernels, attend(): pl.pallas_call(functools.partial(attend_kernel, places, starts, first, la...  30.8 us
    ppermute x15, starting transfers between devices, per_device(): came = ways[way](sent)  28.1 us
    ppermute x15, waiting for transfers between devices, per_device(): came = ways[way](sent)  15.1 us
    pallas_call x1, Pallas kernels, per_device(): query = query_call(normed, query_weight, query_gain, cosine, sine)  2.81 us
    pallas_call x1, Pallas kernels, per_device(): pl.pallas_call(table_kernel, out_shape=(jax.ShapeDtypeStruct((4,), jnp.in...  1.84 us
  transfers between devices with their start and end apart: 16, of which 4 were waited for; matrix products, arithmetic and copies ran while one was open for 0% of the time, Pallas kernels for 41%

profile of v2, /device:TPU:246, one launch (start us, length us, event | category | flops | bytes accessed | tf_op | source)
XLA Modules:
  0.0 81.4 jit_solution(12870568537424168384)
XLA Ops:
  0.0 0.0 copy-start.4
  0.0 0.0 copy-start.5
  0.0 0.0 copy-start.2
  0.0 0.0 copy-start.3
  0.0 0.1 collective-permute-start
  0.1 0.0 copy-start.6
  0.1 0.8 copy-done.6
  0.9 0.0 copy-start.7
  0.9 0.0 copy-start
  0.9 1.8 %tables.1 = (s32[4]{0:T(128)S(1)}, s32[256,128]{1,0:T(8,128)S(1)}, f32[256,128]{1,0:T(8,128)S(1)}, f32[256,128]{1,0:T(8,128)S(1)}) custom-call(s32[32]{0:T(128)S(1)} %copy-done.6), custom_call_target="tpu_custom_call" | custom-call | flops 4294967296 | bytes 12582912 | tf_op jit(solution)/shard_map/tables/pallas_call | solution.py:305
  2.8 0.0 collective-permute-done.other
  2.8 0.0 copy-done.4
  2.8 0.0 copy-done.5
  2.8 0.0 copy-done.2
  2.8 0.0 copy-done.3
  2.8 0.0 copy-done.7
  2.8 0.0 copy-start.1
  2.9 1.3 %keys_values.1 = (bf16[256,2048]{1,0:T(8,128)(2,1)S(1)}, bf16[512,256]{1,0:T(8,128)(2,1)S(1)}) custom-call(bf16[128,2048]{1,0:T(8,128)(2,1)S(1)} %copy-done.4, bf16[128,2048]{1,0:T(8,128)(2,1)S(1)} %collective-permute-done.other, f32[1,2048]{1,0:T(1,128)S(1)} %bitcast.4, bf16[2048,256]{1,0:T(8,128)(2,1)S(1)} %copy-done.2, bf16[2048,256]{1,0:T(8,128)(2,1)S(1)} %copy-done.3, ...), custom_call_target="tpu_custom_call" | custom-call | flops 2147483648 | bytes 6291456 | tf_op jit(solution)/shard_map/keys_values/pallas_call | solution.py:319
  4.1 0.1 collective-permute-start.1
  4.2 8.6 %collective-permute-done.1.refs_2_ = bf16[512,256]{1,0:T(8,128)(2,1)S(1)} collective-permute-done((bf16[512,256]{1,0:T(8,128)(2,1)S(1)}, bf16[512,256]{1,0:T(8,128)(2,1)S(1)}, u32[]{:S(2)}, u32[]{:S(2)}) %collective-permute-start.1) | collective-permute-done | bytes 262176 | tf_op jit(solution)/shard_map/ppermute | solution.py:359
  12.8 3.6 %collective-permute-start.2 = (bf16[512,256]{1,0:T(8,128)(2,1)S(1)}, bf16[512,256]{1,0:T(8,128)(2,1)S(1)}, u32[]{:S(2)}, u32[]{:S(2)}) collective-permute-start(bf16[512,256]{1,0:T(8,128)(2,1)S(1)} %collective-permute-done.1.refs_2_), channel_id=1, source_target_pairs={{0,8},{2,10},{4,12},{6,14},{8,16},{10,18},{12,20},{14,22},{16,24},... | collective-permute-start | bytes 786440 | tf_op jit(solution)/shard_map/ppermute | solution.py:359
  16.4 1.3 %collective-permute-start.13 = (bf16[512,256]{1,0:T(8,128)(2,1)S(1)}, bf16[512,256]{1,0:T(8,128)(2,1)S(1)}, u32[]{:S(2)}, u32[]{:S(2)}) collective-permute-start(bf16[512,256]{1,0:T(8,128)(2,1)S(1)} %get-tuple-element.29.refs_0_), channel_id=1, source_target_pairs={{0,2},{2,4},{4,6},{6,0},{8,10},{10,12},{12,14},{14,8},{16,18},{18,... | collective-permute-start | bytes 786440 | tf_op jit(solution)/shard_map/ppermute | solution.py:359
  17.7 0.7 collective-permute-start.15
  18.4 0.4 collective-permute-start.11
  18.9 0.0 copy-done
  18.9 0.0 copy-done.1
  18.9 2.8 %queries.1.query = bf16[4096,128]{1,0:T(8,128)(2,1)S(1)} custom-call(bf16[256,2048]{1,0:T(8,128)(2,1)S(1)} %get-tuple-element.27.normed, bf16[2048,2048]{1,0:T(8,128)(2,1)S(1)} %copy-done, f32[1,128]{1,0:T(1,128)S(1)} %bitcast.3, f32[256,128]{1,0:T(8,128)S(1)} %get-tuple-element.25.cosine, f32[256,128]{1,0:T(8,128)S(1)} %get-tuple-element.26.sine), custom_call_target="tpu_custom_call" | custom-call | flops 2147483648 | bytes 11534336 | tf_op jit(solution)/shard_map/queries/pallas_call | solution.py:339
  21.7 0.2 collective-permute-done.2.refs_3_
  21.9 5.8 %collective-permute-start.3 = (bf16[512,256]{1,0:T(8,128)(2,1)S(1)}, bf16[512,256]{1,0:T(8,128)(2,1)S(1)}, u32[]{:S(2)}, u32[]{:S(2)}) collective-permute-start(bf16[512,256]{1,0:T(8,128)(2,1)S(1)} %collective-permute-done.2.refs_3_), channel_id=1, source_target_pairs={{0,8},{2,10},{4,12},{6,14},{8,16},{10,18},{12,20},{14,22},{16,24},... | collective-permute-start | bytes 786440 | tf_op jit(solution)/shard_map/ppermute | solution.py:359
  27.7 2.4 %attend.7 = (f32[4096,128]{1,0:T(8,128)S(1)}, f32[4096,128]{1,0:T(8,128)S(1)}) custom-call(s32[4]{0:T(128)S(1)} %get-tuple-element.24.info, bf16[4096,128]{1,0:T(8,128)(2,1)S(1)} %queries.1.query, s32[256,128]{1,0:T(8,128)S(1)} %get-tuple-element.28.opening, bf16[512,256]{1,0:T(8,128)(2,1)S(1)} %get-tuple-element.29.refs_0_), custom_call_target="tpu_custom_call" | custom-call | flops 536870912 | bytes 8388608 | tf_op jit(solution)/shard_map/attend/pallas_call | solution.py:268
  30.2 0.0 collective-permute-done.13.refs_0_
  30.2 1.4 %collective-permute-start.14 = (bf16[1024,256]{1,0:T(8,128)(2,1)S(1)}, bf16[1024,256]{1,0:T(8,128)(2,1)S(1)}, u32[]{:S(2)}, u32[]{:S(2)}) collective-permute-start(bf16[1024,256]{1,0:T(8,128)(2,1)S(1)} %pad_maximum_fusion.3), channel_id=1, source_target_pairs={{0,2},{2,4},{4,6},{6,0},{8,10},{10,12},{12,14},{14,8},{16,18},{18,... | collective-permute-start | bytes 1572872 | tf_op jit(solution)/shard_map/ppermute | solution.py:359
  31.6 0.3 collective-permute-start.9
  31.9 0.0 collective-permute-done.11.refs_2_
  31.9 1.8 %collective-permute-start.12 = (bf16[1024,256]{1,0:T(8,128)(2,1)S(1)}, bf16[1024,256]{1,0:T(8,128)(2,1)S(1)}, u32[]{:S(2)}, u32[]{:S(2)}) collective-permute-start(bf16[1024,256]{1,0:T(8,128)(2,1)S(1)} %pad_maximum_fusion.2), channel_id=1, source_target_pairs={{0,6},{2,0},{4,2},{6,4},{8,14},{10,8},{12,10},{14,12},{16,22},{18,... | collective-permute-start | bytes 1572872 | tf_op jit(solution)/shard_map/ppermute | solution.py:359
  33.8 0.0 collective-permute-done.3.refs_3_
  33.8 4.5 %collective-permute-start.4 = (bf16[512,256]{1,0:T(8,128)(2,1)S(1)}, bf16[512,256]{1,0:T(8,128)(2,1)S(1)}, u32[]{:S(2)}, u32[]{:S(2)}) collective-permute-start(bf16[512,256]{1,0:T(8,128)(2,1)S(1)} %collective-permute-done.3.refs_3_), channel_id=1, source_target_pairs={{0,8},{2,10},{4,12},{6,14},{8,16},{10,18},{12,20},{14,22},{16,24},... | collective-permute-start | bytes 786440 | tf_op jit(solution)/shard_map/ppermute | solution.py:359
  38.2 0.0 collective-permute-done.15.refs_1_
  38.2 0.4 collective-permute-start.7
  38.7 3.7 %attend.8 = (f32[4096,128]{1,0:T(8,128)S(1)}, f32[4096,128]{1,0:T(8,128)S(1)}) custom-call(s32[4]{0:T(128)S(1)} %get-tuple-element.24.info, bf16[4096,128]{1,0:T(8,128)(2,1)S(1)} %queries.1.query, s32[256,128]{1,0:T(8,128)S(1)} %get-tuple-element.28.opening, ...), custom_call_target="tpu_custom_call", output_to_operand_aliasing={{0}: (6, {}), {1}: (7, {})} | custom-call | flops 1610612736 | bytes 8388608 | tf_op jit(solution)/shard_map/attend/pallas_call | solution.py:268
  42.3 6.1 %collective-permute-done.9.refs_1_ = bf16[512,256]{1,0:T(8,128)(2,1)S(1)} collective-permute-done((bf16[512,256]{1,0:T(8,128)(2,1)S(1)}, bf16[512,256]{1,0:T(8,128)(2,1)S(1)}, u32[]{:S(2)}, u32[]{:S(2)}) %collective-permute-start.9) | collective-permute-done | bytes 262176 | tf_op jit(solution)/shard_map/ppermute | solution.py:359
  48.5 1.4 %collective-permute-start.10 = (bf16[1024,256]{1,0:T(8,128)(2,1)S(1)}, bf16[1024,256]{1,0:T(8,128)(2,1)S(1)}, u32[]{:S(2)}, u32[]{:S(2)}) collective-permute-start(bf16[1024,256]{1,0:T(8,128)(2,1)S(1)} %pad_maximum_fusion.1), channel_id=1, source_target_pairs={{0,2},{2,4},{4,6},{6,0},{8,10},{10,12},{12,14},{14,8},{16,18},{18,... | collective-permute-start | bytes 1572872 | tf_op jit(solution)/shard_map/ppermute | solution.py:359
  49.9 0.0 collective-permute-done.4.refs_3_
  49.9 0.0 collective-permute-done.7.refs_2_
  49.9 1.6 %collective-permute-start.8 = (bf16[1024,256]{1,0:T(8,128)(2,1)S(1)}, bf16[1024,256]{1,0:T(8,128)(2,1)S(1)}, u32[]{:S(2)}, u32[]{:S(2)}) collective-permute-start(bf16[1024,256]{1,0:T(8,128)(2,1)S(1)} %pad_maximum_fusion), channel_id=1, source_target_pairs={{0,6},{2,0},{4,2},{6,4},{8,14},{10,8},{12,10},{14,12},{16,22},{18,... | collective-permute-start | bytes 1572872 | tf_op jit(solution)/shard_map/ppermute | solution.py:359
  51.5 1.0 %collective-permute-start.5 = (bf16[512,256]{1,0:T(8,128)(2,1)S(1)}, bf16[512,256]{1,0:T(8,128)(2,1)S(1)}, u32[]{:S(2)}, u32[]{:S(2)}) collective-permute-start(bf16[512,256]{1,0:T(8,128)(2,1)S(1)} %collective-permute-done.4.refs_3_), channel_id=1, source_target_pairs={{0,2},{2,4},{4,6},{6,0},{8,10},{10,12},{12,14},{14,8},{16,18},{18,... | collective-permute-start | bytes 786440 | tf_op jit(solution)/shard_map/ppermute | solution.py:359
  52.5 0.0 collective-permute-done.14.refs_0_.refs_1_
  52.5 6.7 %attend.9 = (f32[4096,128]{1,0:T(8,128)S(1)}, f32[4096,128]{1,0:T(8,128)S(1)}) custom-call(s32[4]{0:T(128)S(1)} %get-tuple-element.24.info, bf16[4096,128]{1,0:T(8,128)(2,1)S(1)} %queries.1.query, s32[256,128]{1,0:T(8,128)S(1)} %get-tuple-element.28.opening, ...), custom_call_target="tpu_custom_call", output_to_operand_aliasing={{0}: (7, {}), {1}: (8, {})} | custom-call | flops 2147483648 | bytes 8388608 | tf_op jit(solution)/shard_map/attend/pallas_call | solution.py:268
  59.2 0.0 collective-permute-done.12.refs_0_.refs_2_
  59.2 6.7 %attend.10 = (f32[4096,128]{1,0:T(8,128)S(1)}, f32[4096,128]{1,0:T(8,128)S(1)}) custom-call(s32[4]{0:T(128)S(1)} %get-tuple-element.24.info, bf16[4096,128]{1,0:T(8,128)(2,1)S(1)} %queries.1.query, s32[256,128]{1,0:T(8,128)S(1)} %get-tuple-element.28.opening, ...), custom_call_target="tpu_custom_call", output_to_operand_aliasing={{0}: (7, {}), {1}: (8, {})} | custom-call | flops 2147483648 | bytes 8388608 | tf_op jit(solution)/shard_map/attend/pallas_call | solution.py:268
  65.9 0.1 collective-permute-done.5.refs_1_
  66.1 3.8 %collective-permute-start.6 = (bf16[512,256]{1,0:T(8,128)(2,1)S(1)}, bf16[512,256]{1,0:T(8,128)(2,1)S(1)}, u32[]{:S(2)}, u32[]{:S(2)}) collective-permute-start(bf16[512,256]{1,0:T(8,128)(2,1)S(1)} %collective-permute-done.5.refs_1_), channel_id=1, source_target_pairs={{0,2},{2,4},{4,6},{6,0},{8,10},{10,12},{12,14},{14,8},{16,18},{18,... | collective-permute-start | bytes 786440 | tf_op jit(solution)/shard_map/ppermute | solution.py:359
  69.8 0.0 collective-permute-done.10.refs_0_.refs_1_
  69.8 5.2 %attend.11 = (f32[4096,128]{1,0:T(8,128)S(1)}, f32[4096,128]{1,0:T(8,128)S(1)}) custom-call(s32[4]{0:T(128)S(1)} %get-tuple-element.24.info, bf16[4096,128]{1,0:T(8,128)(2,1)S(1)} %queries.1.query, s32[256,128]{1,0:T(8,128)S(1)} %get-tuple-element.28.opening, ...), custom_call_target="tpu_custom_call", output_to_operand_aliasing={{0}: (7, {}), {1}: (8, {})} | custom-call | flops 2147483648 | bytes 8388608 | tf_op jit(solution)/shard_map/attend/pallas_call | solution.py:268
  75.0 0.0 collective-permute-done.8.refs_0_.refs_2_
  75.1 4.0 %attend.12 = (f32[4096,128]{1,0:T(8,128)S(1)}, f32[4096,128]{1,0:T(8,128)S(1)}) custom-call(s32[4]{0:T(128)S(1)} %get-tuple-element.24.info, bf16[4096,128]{1,0:T(8,128)(2,1)S(1)} %queries.1.query, s32[256,128]{1,0:T(8,128)S(1)} %get-tuple-element.28.opening, ...), custom_call_target="tpu_custom_call", output_to_operand_aliasing={{0}: (6, {}), {1}: (7, {})} | custom-call | flops 1610612736 | bytes 8388608 | tf_op jit(solution)/shard_map/attend/pallas_call | solution.py:268
  79.0 0.0 collective-permute-done.6.refs_0_
  79.0 2.2 %attend.13 = (f32[4096,128]{1,0:T(8,128)S(1)}, f32[4096,128]{1,0:T(8,128)S(1)}, bf16[256,2048]{1,0:T(8,128)(2,1)}) custom-call(s32[4]{0:T(128)S(1)} %get-tuple-element.24.info, bf16[4096,128]{1,0:T(8,128)(2,1)S(1)} %queries.1.query, s32[256,128]{1,0:T(8,128)S(1)} %get-tuple-element.28.opening, ...), custom_call_target="tpu_custom_call", output_to_operand_aliasing={{0}: (4, {}), {1}: (5, {})} | custom-call | flops 536870912 | bytes 8388608 | tf_op jit(solution)/shard_map/attend/pallas_call | solution.py:268
  (4 shorter events, 0.1 us)
Async XLA Ops:
  0.0 2.8 %copy-start.4 = (bf16[128,2048]{1,0:T(8,128)(2,1)S(1)}, bf16[128,2048]{1,0:T(8,128)(2,1)}, u32[]{:S(2)}) copy-start(bf16[128,2048]{1,0:T(8,128)(2,1)} %own.1) | copy-start | bytes 1572868
  0.0 2.8 %copy-start.5 = (f32[2048]{0:T(1024)S(1)}, f32[2048]{0:T(1024)}, u32[]{:S(2)}) copy-start(f32[2048]{0:T(1024)} %param.9) | copy-start | bytes 24580
  0.0 2.8 %copy-start.2 = (bf16[2048,256]{1,0:T(8,128)(2,1)S(1)}, bf16[2048,256]{1,0:T(8,128)(2,1)}, u32[]{:S(2)}) copy-start(bf16[2048,256]{1,0:T(8,128)(2,1)} %wk.1) | copy-start | bytes 3145732
  0.0 2.8 %copy-start.3 = (bf16[2048,256]{1,0:T(8,128)(2,1)S(1)}, bf16[2048,256]{1,0:T(8,128)(2,1)}, u32[]{:S(2)}) copy-start(bf16[2048,256]{1,0:T(8,128)(2,1)} %wv.1) | copy-start | bytes 3145732
  0.0 2.8 %collective-permute-start = (bf16[128,2048]{1,0:T(8,128)(2,1)}, bf16[128,2048]{1,0:T(8,128)(2,1)S(1)}, u32[]{:S(2)}, u32[]{:S(2)}) collective-permute-start(bf16[128,2048]{1,0:T(8,128)(2,1)} %own.1), channel_id=1, source_target_pairs={{0,1},{1,0},{2,3},{3,2},{4,5},{5,4},{6,7},{7,6},{8,9},{9,8},{10,11... | collective-permute-start | bytes 1572872 | tf_op jit(solution)/shard_map/ppermute | solution.py:300
  0.1 0.8 copy-start.6
  0.9 1.9 %copy-start.7 = (f32[128]{0:T(128)S(1)}, f32[128]{0:T(128)}, u32[]{:S(2)}) copy-start(f32[128]{0:T(128)} %param.14) | copy-start | bytes 1540
  0.9 18.0 %copy-start = (bf16[2048,2048]{1,0:T(8,128)(2,1)S(1)}, bf16[2048,2048]{1,0:T(8,128)(2,1)}, u32[]{:S(2)}) copy-start(bf16[2048,2048]{1,0:T(8,128)(2,1)} %wq.1) | copy-start | bytes 25165828
  2.8 16.0 %copy-start.1 = (f32[128]{0:T(128)S(1)}, f32[128]{0:T(128)}, u32[]{:S(2)}) copy-start(f32[128]{0:T(128)} %param.13) | copy-start | bytes 1540
  4.1 8.7 %collective-permute-start.1 = (bf16[512,256]{1,0:T(8,128)(2,1)S(1)}, bf16[512,256]{1,0:T(8,128)(2,1)S(1)}, u32[]{:S(2)}, u32[]{:S(2)}) collective-permute-start(bf16[512,256]{1,0:T(8,128)(2,1)S(1)} %get-tuple-element.29.refs_0_), channel_id=1, source_target_pairs={{0,8},{2,10},{4,12},{6,14},{8,16},{10,18},{12,20},{14,22},{16,24},... | collective-permute-start | bytes 786440 | tf_op jit(solution)/shard_map/ppermute | solution.py:359
  12.8 9.1 %collective-permute-start.2 = (bf16[512,256]{1,0:T(8,128)(2,1)S(1)}, bf16[512,256]{1,0:T(8,128)(2,1)S(1)}, u32[]{:S(2)}, u32[]{:S(2)}) collective-permute-start(bf16[512,256]{1,0:T(8,128)(2,1)S(1)} %collective-permute-done.1.refs_2_), channel_id=1, source_target_pairs={{0,8},{2,10},{4,12},{6,14},{8,16},{10,18},{12,20},{14,22},{16,24},... | collective-permute-start | bytes 786440 | tf_op jit(solution)/shard_map/ppermute | solution.py:359
  16.4 13.8 %collective-permute-start.13 = (bf16[512,256]{1,0:T(8,128)(2,1)S(1)}, bf16[512,256]{1,0:T(8,128)(2,1)S(1)}, u32[]{:S(2)}, u32[]{:S(2)}) collective-permute-start(bf16[512,256]{1,0:T(8,128)(2,1)S(1)} %get-tuple-element.29.refs_0_), channel_id=1, source_target_pairs={{0,2},{2,4},{4,6},{6,0},{8,10},{10,12},{12,14},{14,8},{16,18},{18,... | collective-permute-start | bytes 786440 | tf_op jit(solution)/shard_map/ppermute | solution.py:359
  17.7 20.5 %collective-permute-start.15 = (bf16[512,256]{1,0:T(8,128)(2,1)S(1)}, bf16[512,256]{1,0:T(8,128)(2,1)S(1)}, u32[]{:S(2)}, u32[]{:S(2)}) collective-permute-start(bf16[512,256]{1,0:T(8,128)(2,1)S(1)} %get-tuple-element.29.refs_0_), channel_id=1, source_target_pairs={{0,6},{2,0},{4,2},{6,4},{8,14},{10,8},{12,10},{14,12},{16,22},{18,... | collective-permute-start | bytes 786440 | tf_op jit(solution)/shard_map/ppermute | solution.py:359
  18.4 13.5 %collective-permute-start.11 = (bf16[512,256]{1,0:T(8,128)(2,1)S(1)}, bf16[512,256]{1,0:T(8,128)(2,1)S(1)}, u32[]{:S(2)}, u32[]{:S(2)}) collective-permute-start(bf16[512,256]{1,0:T(8,128)(2,1)S(1)} %collective-permute-done.1.refs_2_), channel_id=1, source_target_pairs={{0,6},{2,0},{4,2},{6,4},{8,14},{10,8},{12,10},{14,12},{16,22},{18,... | collective-permute-start | bytes 786440 | tf_op jit(solution)/shard_map/ppermute | solution.py:359
  21.9 11.8 %collective-permute-start.3 = (bf16[512,256]{1,0:T(8,128)(2,1)S(1)}, bf16[512,256]{1,0:T(8,128)(2,1)S(1)}, u32[]{:S(2)}, u32[]{:S(2)}) collective-permute-start(bf16[512,256]{1,0:T(8,128)(2,1)S(1)} %collective-permute-done.2.refs_3_), channel_id=1, source_target_pairs={{0,8},{2,10},{4,12},{6,14},{8,16},{10,18},{12,20},{14,22},{16,24},... | collective-permute-start | bytes 786440 | tf_op jit(solution)/shard_map/ppermute | solution.py:359
  30.2 22.2 %collective-permute-start.14 = (bf16[1024,256]{1,0:T(8,128)(2,1)S(1)}, bf16[1024,256]{1,0:T(8,128)(2,1)S(1)}, u32[]{:S(2)}, u32[]{:S(2)}) collective-permute-start(bf16[1024,256]{1,0:T(8,128)(2,1)S(1)} %pad_maximum_fusion.3), channel_id=1, source_target_pairs={{0,2},{2,4},{4,6},{6,0},{8,10},{10,12},{12,14},{14,8},{16,18},{18,... | collective-permute-start | bytes 1572872 | tf_op jit(solution)/shard_map/ppermute | solution.py:359
  31.6 16.8 %collective-permute-start.9 = (bf16[512,256]{1,0:T(8,128)(2,1)S(1)}, bf16[512,256]{1,0:T(8,128)(2,1)S(1)}, u32[]{:S(2)}, u32[]{:S(2)}) collective-permute-start(bf16[512,256]{1,0:T(8,128)(2,1)S(1)} %collective-permute-done.2.refs_3_), channel_id=1, source_target_pairs={{0,2},{2,4},{4,6},{6,0},{8,10},{10,12},{12,14},{14,8},{16,18},{18,... | collective-permute-start | bytes 786440 | tf_op jit(solution)/shard_map/ppermute | solution.py:359
  31.9 27.3 %collective-permute-start.12 = (bf16[1024,256]{1,0:T(8,128)(2,1)S(1)}, bf16[1024,256]{1,0:T(8,128)(2,1)S(1)}, u32[]{:S(2)}, u32[]{:S(2)}) collective-permute-start(bf16[1024,256]{1,0:T(8,128)(2,1)S(1)} %pad_maximum_fusion.2), channel_id=1, source_target_pairs={{0,6},{2,0},{4,2},{6,4},{8,14},{10,8},{12,10},{14,12},{16,22},{18,... | collective-permute-start | bytes 1572872 | tf_op jit(solution)/shard_map/ppermute | solution.py:359
  33.8 16.1 %collective-permute-start.4 = (bf16[512,256]{1,0:T(8,128)(2,1)S(1)}, bf16[512,256]{1,0:T(8,128)(2,1)S(1)}, u32[]{:S(2)}, u32[]{:S(2)}) collective-permute-start(bf16[512,256]{1,0:T(8,128)(2,1)S(1)} %collective-permute-done.3.refs_3_), channel_id=1, source_target_pairs={{0,8},{2,10},{4,12},{6,14},{8,16},{10,18},{12,20},{14,22},{16,24},... | collective-permute-start | bytes 786440 | tf_op jit(solution)/shard_map/ppermute | solution.py:359
  38.2 11.6 %collective-permute-start.7 = (bf16[512,256]{1,0:T(8,128)(2,1)S(1)}, bf16[512,256]{1,0:T(8,128)(2,1)S(1)}, u32[]{:S(2)}, u32[]{:S(2)}) collective-permute-start(bf16[512,256]{1,0:T(8,128)(2,1)S(1)} %collective-permute-done.3.refs_3_), channel_id=1, source_target_pairs={{0,6},{2,0},{4,2},{6,4},{8,14},{10,8},{12,10},{14,12},{16,22},{18,... | collective-permute-start | bytes 786440 | tf_op jit(solution)/shard_map/ppermute | solution.py:359
  48.5 21.4 %collective-permute-start.10 = (bf16[1024,256]{1,0:T(8,128)(2,1)S(1)}, bf16[1024,256]{1,0:T(8,128)(2,1)S(1)}, u32[]{:S(2)}, u32[]{:S(2)}) collective-permute-start(bf16[1024,256]{1,0:T(8,128)(2,1)S(1)} %pad_maximum_fusion.1), channel_id=1, source_target_pairs={{0,2},{2,4},{4,6},{6,0},{8,10},{10,12},{12,14},{14,8},{16,18},{18,... | collective-permute-start | bytes 1572872 | tf_op jit(solution)/shard_map/ppermute | solution.py:359
  49.9 25.1 %collective-permute-start.8 = (bf16[1024,256]{1,0:T(8,128)(2,1)S(1)}, bf16[1024,256]{1,0:T(8,128)(2,1)S(1)}, u32[]{:S(2)}, u32[]{:S(2)}) collective-permute-start(bf16[1024,256]{1,0:T(8,128)(2,1)S(1)} %pad_maximum_fusion), channel_id=1, source_target_pairs={{0,6},{2,0},{4,2},{6,4},{8,14},{10,8},{12,10},{14,12},{16,22},{18,... | collective-permute-start | bytes 1572872 | tf_op jit(solution)/shard_map/ppermute | solution.py:359
  51.5 14.6 %collective-permute-start.5 = (bf16[512,256]{1,0:T(8,128)(2,1)S(1)}, bf16[512,256]{1,0:T(8,128)(2,1)S(1)}, u32[]{:S(2)}, u32[]{:S(2)}) collective-permute-start(bf16[512,256]{1,0:T(8,128)(2,1)S(1)} %collective-permute-done.4.refs_3_), channel_id=1, source_target_pairs={{0,2},{2,4},{4,6},{6,0},{8,10},{10,12},{12,14},{14,8},{16,18},{18,... | collective-permute-start | bytes 786440 | tf_op jit(solution)/shard_map/ppermute | solution.py:359
  66.1 13.0 %collective-permute-start.6 = (bf16[512,256]{1,0:T(8,128)(2,1)S(1)}, bf16[512,256]{1,0:T(8,128)(2,1)S(1)}, u32[]{:S(2)}, u32[]{:S(2)}) collective-permute-start(bf16[512,256]{1,0:T(8,128)(2,1)S(1)} %collective-permute-done.5.refs_1_), channel_id=1, source_target_pairs={{0,2},{2,4},{4,6},{6,0},{8,10},{10,12},{12,14},{14,8},{16,18},{18,... | collective-permute-start | bytes 786440 | tf_op jit(solution)/shard_map/ppermute | solution.py:359

commit v3 on v2

--- a/solution.py
+++ b/solution.py
@@ -20,7 +20,7 @@
 WHOLE = pl.BlockSpec(memory_space=VMEM)
 SCALARS = pl.BlockSpec(memory_space=SMEM)
 PARAMS = pltpu.CompilerParams(vmem_limit_bytes=24 * 1024 * 1024)
-STACK = 2
+STACK = 4
 
 
 MOVES = (
@@ -46,9 +46,13 @@
     ),
     (
         ("up", ((4, 0),), ((4, -1),)),
-        ("down", ((3, 1), (4, 0)), ((3, 2), (4, 1))),
-    ),
-    (("up", ((4, -1),), ((4, 2),)),),
+        ("down", ((4, 0),), ((4, 1),)),
+        ("down", ((3, 1),), ((3, 2),)),
+    ),
+    (
+        ("up", ((4, -1),), ((4, 2),)),
+        ("down", ((4, 1),), ((4, 2),)),
+    ),
 )
 USES = (
     ((0, 0),),
@@ -166,8 +170,9 @@
 
 def attend_kernel(places, starts, first, last, heads, info, query, opening, *refs):
     count = len(places)
-    chunks = refs[:count]
-    refs = refs[count if first else count + 2 :]
+    arrays = sum(len(pieces) for pieces in starts)
+    chunks = refs[:arrays]
+    refs = refs[arrays if first else arrays + 2 :]
     acc, den = refs[:2]
     held, bias, fars, sems = refs[-4:]
     dim = query.shape[1]
@@ -177,15 +182,23 @@
     first_row = shard * rows
     reach = shard - lax.div(lowest, rows)
 
+    upcoming = iter(chunks)
     for index, (level, offset) in enumerate(places):
+        sources = [next(upcoming) for _ in starts[index]]
         far = RING * level + column - lax.rem(column + offset + RING, RING)
         wanted = (far >= 0) & (far <= reach)
         fars[index] = jnp.where(wanted, far, -1)
 
         @pl.when(wanted)
         def _():
-            block = chunks[index].at[pl.ds(starts[index], 2 * rows), :]
-            pltpu.make_async_copy(block, held.at[index], sems.at[index]).start()
+            to = 0
+            for source, (start, part) in zip(sources, starts[index], strict=True):
+                pltpu.make_async_copy(
+                    source.at[pl.ds(start, part), :],
+                    held.at[index, pl.ds(to, part), :],
+                    sems.at[index],
+                ).start()
+                to += part
 
     if first:
         acc[...] = jnp.zeros_like(acc)
@@ -246,11 +259,20 @@
 
     lax.fori_loop(0, count, step, 0)
     if last:
-        out = refs[2]
+        out, ready, out_sems = refs[2:5]
+        copies = []
         for head in range(heads):
             part = pl.ds(head * rows, rows)
             share = 1.0 / jnp.sum(den[part, :], axis=-1, keepdims=True)
-            out[:, head * dim : (head + 1) * dim] = (acc[part, :] * share).astype(jnp.bfloat16)
+            ready[:, head * dim : (head + 1) * dim] = (acc[part, :] * share).astype(jnp.bfloat16)
+            if (head + 1) % 4 == 0:
+                cols = (slice(None), slice((head - 3) * dim, (head + 1) * dim))
+                copies.append(
+                    pltpu.make_async_copy(ready.at[cols], out.at[cols], out_sems.at[head // 4])
+                )
+                copies[-1].start()
+        for copy in copies:
+            copy.wait()
 
 
 def attend(places, blocks, size, info, query, opening, carried, last, heads):
@@ -258,8 +280,8 @@
     rows = stacked // heads
     first = carried is None
     count = len(places)
-    chunks = [chunk for chunk, _ in blocks]
-    starts = [start for _, start in blocks]
+    chunks = [array for pieces in blocks for array, _, _ in pieces]
+    starts = [[(start, rows_of) for _, start, rows_of in pieces] for pieces in blocks]
     state = jax.ShapeDtypeStruct((stacked, dim), jnp.float32)
     out_shape = (state, state)
     if last:
@@ -269,11 +291,16 @@
         functools.partial(attend_kernel, places, starts, first, last, heads),
         out_shape=out_shape,
         in_specs=[SCALARS, WHOLE, WHOLE]
-        + [pl.BlockSpec(memory_space=pl.ANY)] * count
+        + [pl.BlockSpec(memory_space=pl.ANY)] * len(chunks)
         + ([] if first else [WHOLE, WHOLE]),
-        out_specs=(WHOLE,) * len(out_shape),
-        input_output_aliases={} if first else {3 + count: 0, 4 + count: 1},
-        scratch_shapes=[
+        out_specs=(WHOLE, WHOLE, pl.BlockSpec(memory_space=pl.ANY))[: len(out_shape)],
+        input_output_aliases={} if first else {3 + len(chunks): 0, 4 + len(chunks): 1},
+        scratch_shapes=(
+            [VMEM((rows, heads * dim), jnp.bfloat16), pltpu.SemaphoreType.DMA((heads // 4,))]
+            if last
+            else []
+        )
+        + [
             VMEM((count, size, chunks[0].shape[1]), jnp.bfloat16),
             VMEM((rows, rows), jnp.float32),
             SMEM((count,), jnp.int32),
@@ -350,15 +377,21 @@
     )
 
     ways = {"up": up, "down": down, "ahead": ahead}
-    held = {(0, 0): (kv, 0)}
     size = kv.shape[0]
+    held = {(0, 0): [(kv, 0, size)]}
     for moves in MOVES:
+        targets = [place for _, _, places in moves for place in places]
         for way, sources, places in moves:
-            blocks = [held[p][0] for p in sources]
+            shared = targets.count(places[0])
+            rows_of = size // shared
+            blocks = [held[p][0][0] for p in sources]
+            if shared > 1:
+                at = rows_of * len(held.get(places[0], ()))
+                blocks = [block[at : at + rows_of] for block in blocks]
             sent = blocks[0] if len(blocks) == 1 else jnp.concatenate(blocks, axis=0)
             came = ways[way](sent)
             for index, place in enumerate(places):
-                held[place] = (came, index * size)
+                held.setdefault(place, []).append((came, index * rows_of, rows_of))
 
     def use(places, carried, last):
         blocks = [held[p] for p in places]

time: 81.5 us -> 79.2 us (0.972)
  the two profiles are of different devices: /device:TPU:246 before, /device:TPU:230 now
where the time goes in v3:
time: 79.2 us; the launch traced here: 79.1 us
  starting transfers between devices  35.4 us (45%)
  Pallas kernels  33.3 us (42%)
  waiting for transfers between devices  9 us (11%)
  local copies, waits for them, and re-layouts  0.85 us (1%)
    ppermute x17, starting transfers between devices, per_device(): came = ways[way](sent)  35.3 us
    pallas_call x7, Pallas kernels, attend(): pl.pallas_call(functools.partial(attend_kernel, places, starts, first, la...  27.4 us
    ppermute x17, waiting for transfers between devices, per_device(): came = ways[way](sent)  9 us
    pallas_call x1, Pallas kernels, per_device(): query = query_call(normed, query_weight, query_gain, cosine, sine)  2.81 us
    pallas_call x1, Pallas kernels, per_device(): pl.pallas_call(table_kernel, out_shape=(jax.ShapeDtypeStruct((4,), jnp.in...  1.84 us
  transfers between devices with their start and end apart: 18, of which 3 were waited for; matrix products, arithmetic and copies ran while one was open for 0% of the time, Pallas kernels for 38%

profile of v3, /device:TPU:230, one launch (start us, length us, event | category | flops | bytes accessed | tf_op | source)
XLA Modules:
  0.0 79.1 jit_solution(18419421813610567698)
XLA Ops:
  0.0 0.0 copy-start.4
  0.0 0.0 copy-start.5
  0.0 0.0 copy-start.2
  0.0 0.0 copy-start.3
  0.0 0.1 collective-permute-start
  0.1 0.0 copy-start.6
  0.1 0.8 %copy-done.6 = s32[32]{0:T(128)S(1)} copy-done((s32[32]{0:T(128)S(1)}, s32[32]{0:T(128)}, u32[]{:S(2)}) %copy-start.6) | copy-done | bytes 152
  0.9 0.0 copy-start.7
  0.9 1.8 %tables.1 = (s32[4]{0:T(128)S(1)}, s32[256,128]{1,0:T(8,128)S(1)}, f32[256,128]{1,0:T(8,128)S(1)}, f32[256,128]{1,0:T(8,128)S(1)}) custom-call(s32[32]{0:T(128)S(1)} %copy-done.6), custom_call_target="tpu_custom_call" | custom-call | flops 4294967296 | bytes 12582912 | tf_op jit(solution)/shard_map/tables/pallas_call | solution.py:332
  2.8 0.0 collective-permute-done.other
  2.8 0.0 copy-done.4
  2.8 0.0 copy-done.5
  2.8 0.0 copy-done.2
  2.8 0.0 copy-done.3
  2.8 0.0 copy-done.7
  2.8 0.0 copy-start
  2.9 0.0 copy-start.1
  2.9 1.3 %keys_values.1 = (bf16[256,2048]{1,0:T(8,128)(2,1)S(1)}, bf16[512,256]{1,0:T(8,128)(2,1)S(1)}) custom-call(bf16[128,2048]{1,0:T(8,128)(2,1)S(1)} %copy-done.4, bf16[128,2048]{1,0:T(8,128)(2,1)S(1)} %collective-permute-done.other, f32[1,2048]{1,0:T(1,128)S(1)} %bitcast.4, bf16[2048,256]{1,0:T(8,128)(2,1)S(1)} %copy-done.2, bf16[2048,256]{1,0:T(8,128)(2,1)S(1)} %copy-done.3, ...), custom_call_target="tpu_custom_call" | custom-call | flops 2147483648 | bytes 6291456 | tf_op jit(solution)/shard_map/keys_values/pallas_call | solution.py:346
  4.1 0.1 collective-permute-start.1
  4.2 1.7 %collective-permute-start.15 = (bf16[512,256]{1,0:T(8,128)(2,1)S(1)}, bf16[512,256]{1,0:T(8,128)(2,1)S(1)}, u32[]{:S(2)}, u32[]{:S(2)}) collective-permute-start(bf16[512,256]{1,0:T(8,128)(2,1)S(1)} %get-tuple-element.29.refs_0_), channel_id=1, source_target_pairs={{0,2},{2,4},{4,6},{6,0},{8,10},{10,12},{12,14},{14,8},{16,18},{18,... | collective-permute-start | bytes 786440 | tf_op jit(solution)/shard_map/ppermute | solution.py:392
  5.9 6.9 %collective-permute-done.1.refs_2_ = bf16[512,256]{1,0:T(8,128)(2,1)S(1)} collective-permute-done((bf16[512,256]{1,0:T(8,128)(2,1)S(1)}, bf16[512,256]{1,0:T(8,128)(2,1)S(1)}, u32[]{:S(2)}, u32[]{:S(2)}) %collective-permute-start.1) | collective-permute-done | bytes 262176 | tf_op jit(solution)/shard_map/ppermute | solution.py:392
  12.8 3.6 %collective-permute-start.2 = (bf16[512,256]{1,0:T(8,128)(2,1)S(1)}, bf16[512,256]{1,0:T(8,128)(2,1)S(1)}, u32[]{:S(2)}, u32[]{:S(2)}) collective-permute-start(bf16[512,256]{1,0:T(8,128)(2,1)S(1)} %collective-permute-done.1.refs_2_), channel_id=1, source_target_pairs={{0,8},{2,10},{4,12},{6,14},{8,16},{10,18},{12,20},{14,22},{16,24},... | collective-permute-start | bytes 786440 | tf_op jit(solution)/shard_map/ppermute | solution.py:392
  16.4 3.0 %collective-permute-start.17 = (bf16[512,256]{1,0:T(8,128)(2,1)S(1)}, bf16[512,256]{1,0:T(8,128)(2,1)S(1)}, u32[]{:S(2)}, u32[]{:S(2)}) collective-permute-start(bf16[512,256]{1,0:T(8,128)(2,1)S(1)} %get-tuple-element.29.refs_0_), channel_id=1, source_target_pairs={{0,6},{2,0},{4,2},{6,4},{8,14},{10,8},{12,10},{14,12},{16,22},{18,... | collective-permute-start | bytes 786440 | tf_op jit(solution)/shard_map/ppermute | solution.py:392
  19.4 0.7 collective-permute-start.13
  20.2 0.0 collective-permute-done.15.refs_0_
  20.2 1.4 %collective-permute-start.16 = (bf16[1024,256]{1,0:T(8,128)(2,1)S(1)}, bf16[1024,256]{1,0:T(8,128)(2,1)S(1)}, u32[]{:S(2)}, u32[]{:S(2)}) collective-permute-start(bf16[1024,256]{1,0:T(8,128)(2,1)S(1)} %pad_maximum_fusion.2), channel_id=1, source_target_pairs={{0,2},{2,4},{4,6},{6,0},{8,10},{10,12},{12,14},{14,8},{16,18},{18,... | collective-permute-start | bytes 1572872 | tf_op jit(solution)/shard_map/ppermute | solution.py:392
  21.6 0.4 collective-permute-done.2.refs_3_
  22.0 5.8 %collective-permute-start.3 = (bf16[512,256]{1,0:T(8,128)(2,1)S(1)}, bf16[512,256]{1,0:T(8,128)(2,1)S(1)}, u32[]{:S(2)}, u32[]{:S(2)}) collective-permute-start(bf16[512,256]{1,0:T(8,128)(2,1)S(1)} %collective-permute-done.2.refs_3_), channel_id=1, source_target_pairs={{0,8},{2,10},{4,12},{6,14},{8,16},{10,18},{12,20},{14,22},{16,24},... | collective-permute-start | bytes 786440 | tf_op jit(solution)/shard_map/ppermute | solution.py:392
  27.8 1.6 %collective-permute-start.11 = (bf16[512,256]{1,0:T(8,128)(2,1)S(1)}, bf16[512,256]{1,0:T(8,128)(2,1)S(1)}, u32[]{:S(2)}, u32[]{:S(2)}) collective-permute-start(bf16[512,256]{1,0:T(8,128)(2,1)S(1)} %collective-permute-done.2.refs_3_), channel_id=1, source_target_pairs={{0,2},{2,4},{4,6},{6,0},{8,10},{10,12},{12,14},{14,8},{16,18},{18,... | collective-permute-start | bytes 786440 | tf_op jit(solution)/shard_map/ppermute | solution.py:392
  29.3 0.0 copy-done
  29.3 0.0 copy-done.1
  29.3 2.8 %queries.1.query = bf16[4096,128]{1,0:T(8,128)(2,1)S(1)} custom-call(bf16[256,2048]{1,0:T(8,128)(2,1)S(1)} %get-tuple-element.27.normed, bf16[2048,2048]{1,0:T(8,128)(2,1)S(1)} %copy-done, f32[1,128]{1,0:T(1,128)S(1)} %bitcast.3, f32[256,128]{1,0:T(8,128)S(1)} %get-tuple-element.25.cosine, f32[256,128]{1,0:T(8,128)S(1)} %get-tuple-element.26.sine), custom_call_target="tpu_custom_call" | custom-call | flops 2147483648 | bytes 11534336 | tf_op jit(solution)/shard_map/queries/pallas_call | solution.py:366
  32.1 0.0 collective-permute-done.13.refs_2_
  32.2 1.9 %collective-permute-start.14 = (bf16[1024,256]{1,0:T(8,128)(2,1)S(1)}, bf16[1024,256]{1,0:T(8,128)(2,1)S(1)}, u32[]{:S(2)}, u32[]{:S(2)}) collective-permute-start(bf16[1024,256]{1,0:T(8,128)(2,1)S(1)} %pad_maximum_fusion.1), channel_id=1, source_target_pairs={{0,6},{2,0},{4,2},{6,4},{8,14},{10,8},{12,10},{14,12},{16,22},{18,... | collective-permute-start | bytes 1572872 | tf_op jit(solution)/shard_map/ppermute | solution.py:392
  34.1 2.6 %attend.7 = (f32[4096,128]{1,0:T(8,128)S(1)}, f32[4096,128]{1,0:T(8,128)S(1)}) custom-call(s32[4]{0:T(128)S(1)} %get-tuple-element.24.info, bf16[4096,128]{1,0:T(8,128)(2,1)S(1)} %queries.1.query, s32[256,128]{1,0:T(8,128)S(1)} %get-tuple-element.28.opening, bf16[512,256]{1,0:T(8,128)(2,1)S(1)} %get-tuple-element.29.refs_0_), custom_call_target="tpu_custom_call" | custom-call | flops 536870912 | bytes 8388608 | tf_op jit(solution)/shard_map/attend/pallas_call | solution.py:290
  36.7 0.0 collective-permute-done.3.refs_3_
  36.7 1.6 %collective-permute-start.4 = (bf16[512,256]{1,0:T(8,128)(2,1)S(1)}, bf16[512,256]{1,0:T(8,128)(2,1)S(1)}, u32[]{:S(2)}, u32[]{:S(2)}) collective-permute-start(bf16[512,256]{1,0:T(8,128)(2,1)S(1)} %collective-permute-done.3.refs_3_), channel_id=1, source_target_pairs={{0,8},{2,10},{4,12},{6,14},{8,16},{10,18},{12,20},{14,22},{16,24},... | collective-permute-start | bytes 786440 | tf_op jit(solution)/shard_map/ppermute | solution.py:392
  38.3 1.6 %collective-permute-done.11.refs_1_ = bf16[512,256]{1,0:T(8,128)(2,1)S(1)} collective-permute-done((bf16[512,256]{1,0:T(8,128)(2,1)S(1)}, bf16[512,256]{1,0:T(8,128)(2,1)S(1)}, u32[]{:S(2)}, u32[]{:S(2)}) %collective-permute-start.11) | collective-permute-done | bytes 262176 | tf_op jit(solution)/shard_map/ppermute | solution.py:392
  39.9 0.1 collective-permute-start.12
  40.1 0.0 collective-permute-done.17.refs_1_
  40.1 3.2 %collective-permute-start.9 = (bf16[512,256]{1,0:T(8,128)(2,1)S(1)}, bf16[512,256]{1,0:T(8,128)(2,1)S(1)}, u32[]{:S(2)}, u32[]{:S(2)}) collective-permute-start(bf16[512,256]{1,0:T(8,128)(2,1)S(1)} %collective-permute-done.3.refs_3_), channel_id=1, source_target_pairs={{0,6},{2,0},{4,2},{6,4},{8,14},{10,8},{12,10},{14,12},{16,22},{18,... | collective-permute-start | bytes 786440 | tf_op jit(solution)/shard_map/ppermute | solution.py:392
  43.3 2.1 %attend.8 = (f32[4096,128]{1,0:T(8,128)S(1)}, f32[4096,128]{1,0:T(8,128)S(1)}) custom-call(s32[4]{0:T(128)S(1)} %get-tuple-element.24.info, bf16[4096,128]{1,0:T(8,128)(2,1)S(1)} %queries.1.query, s32[256,128]{1,0:T(8,128)S(1)} %get-tuple-element.28.opening, ...), custom_call_target="tpu_custom_call", output_to_operand_aliasing={{0}: (6, {}), {1}: (7, {})} | custom-call | flops 1610612736 | bytes 8388608 | tf_op jit(solution)/shard_map/attend/pallas_call | solution.py:290
  45.4 0.0 collective-permute-done.4.refs_3_
  45.4 0.4 collective-permute-start.5
  45.9 0.0 collective-permute-done.16.refs_0_.refs_1_
  45.9 3.1 %collective-permute-start.7 = (bf16[512,256]{1,0:T(8,128)(2,1)S(1)}, bf16[512,256]{1,0:T(8,128)(2,1)S(1)}, u32[]{:S(2)}, u32[]{:S(2)}) collective-permute-start(bf16[512,256]{1,0:T(8,128)(2,1)S(1)} %collective-permute-done.4.refs_3_), channel_id=1, source_target_pairs={{0,6},{2,0},{4,2},{6,4},{8,14},{10,8},{12,10},{14,12},{16,22},{18,... | collective-permute-start | bytes 786440 | tf_op jit(solution)/shard_map/ppermute | solution.py:392
  48.9 5.1 %attend.9 = (f32[4096,128]{1,0:T(8,128)S(1)}, f32[4096,128]{1,0:T(8,128)S(1)}) custom-call(s32[4]{0:T(128)S(1)} %get-tuple-element.24.info, bf16[4096,128]{1,0:T(8,128)(2,1)S(1)} %queries.1.query, s32[256,128]{1,0:T(8,128)S(1)} %get-tuple-element.28.opening, ...), custom_call_target="tpu_custom_call", output_to_operand_aliasing={{0}: (7, {}), {1}: (8, {})} | custom-call | flops 2147483648 | bytes 8388608 | tf_op jit(solution)/shard_map/attend/pallas_call | solution.py:290
  54.0 0.0 collective-permute-done.9.refs_2_
  54.0 3.8 %collective-permute-start.10 = (bf16[512,256]{1,0:T(8,128)(2,1)S(1)}, bf16[512,256]{1,0:T(8,128)(2,1)S(1)}, u32[]{:S(2)}, u32[]{:S(2)}) collective-permute-start(bf16[512,256]{1,0:T(8,128)(2,1)S(1)} %collective-permute-done.9.refs_2_), channel_id=1, source_target_pairs={{0,6},{2,0},{4,2},{6,4},{8,14},{10,8},{12,10},{14,12},{16,22},{18,... | collective-permute-start | bytes 786440 | tf_op jit(solution)/shard_map/ppermute | solution.py:392
  57.9 0.0 collective-permute-done.14.refs_0_.refs_2_
  57.9 6.6 %attend.10 = (f32[4096,128]{1,0:T(8,128)S(1)}, f32[4096,128]{1,0:T(8,128)S(1)}) custom-call(s32[4]{0:T(128)S(1)} %get-tuple-element.24.info, bf16[4096,128]{1,0:T(8,128)(2,1)S(1)} %queries.1.query, s32[256,128]{1,0:T(8,128)S(1)} %get-tuple-element.28.opening, ...), custom_call_target="tpu_custom_call", output_to_operand_aliasing={{0}: (7, {}), {1}: (8, {})} | custom-call | flops 2147483648 | bytes 8388608 | tf_op jit(solution)/shard_map/attend/pallas_call | solution.py:290
  64.5 0.0 collective-permute-done.5.refs_1_
  64.5 0.1 collective-permute-start.6
  64.6 0.0 collective-permute-done.7.refs_2_
  64.6 3.3 %collective-permute-start.8 = (bf16[256,256]{1,0:T(8,128)(2,1)S(1)}, bf16[256,256]{1,0:T(8,128)(2,1)S(1)}, u32[]{:S(2)}, u32[]{:S(2)}) collective-permute-start(bf16[256,256]{1,0:T(8,128)(2,1)S(1)} %slice.9), channel_id=1, source_target_pairs={{0,6},{2,0},{4,2},{6,4},{8,14},{10,8},{12,10},{14,12},{16,22},{18,... | collective-permute-start | bytes 393224 | tf_op jit(solution)/shard_map/ppermute | solution.py:392
  67.9 0.0 collective-permute-done.12.refs_0_.refs_1_
  67.9 5.1 %attend.11 = (f32[4096,128]{1,0:T(8,128)S(1)}, f32[4096,128]{1,0:T(8,128)S(1)}) custom-call(s32[4]{0:T(128)S(1)} %get-tuple-element.24.info, bf16[4096,128]{1,0:T(8,128)(2,1)S(1)} %queries.1.query, s32[256,128]{1,0:T(8,128)S(1)} %get-tuple-element.28.opening, ...), custom_call_target="tpu_custom_call", output_to_operand_aliasing={{0}: (7, {}), {1}: (8, {})} | custom-call | flops 2147483648 | bytes 8388608 | tf_op jit(solution)/shard_map/attend/pallas_call | solution.py:290
  73.0 0.0 collective-permute-done.10.refs_0_
  73.0 3.9 %attend.12 = (f32[4096,128]{1,0:T(8,128)S(1)}, f32[4096,128]{1,0:T(8,128)S(1)}) custom-call(s32[4]{0:T(128)S(1)} %get-tuple-element.24.info, bf16[4096,128]{1,0:T(8,128)(2,1)S(1)} %queries.1.query, s32[256,128]{1,0:T(8,128)S(1)} %get-tuple-element.28.opening, ...), custom_call_target="tpu_custom_call", output_to_operand_aliasing={{0}: (6, {}), {1}: (7, {})} | custom-call | flops 1610612736 | bytes 8388608 | tf_op jit(solution)/shard_map/attend/pallas_call | solution.py:290
  77.0 0.0 collective-permute-done.6.refs_0_
  77.0 0.0 collective-permute-done.8.refs_1_
  77.0 1.9 %attend.13 = (f32[4096,128]{1,0:T(8,128)S(1)}, f32[4096,128]{1,0:T(8,128)S(1)}, bf16[256,2048]{1,0:T(8,128)(2,1)}) custom-call(s32[4]{0:T(128)S(1)} %get-tuple-element.24.info, bf16[4096,128]{1,0:T(8,128)(2,1)S(1)} %queries.1.query, s32[256,128]{1,0:T(8,128)S(1)} %get-tuple-element.28.opening, ...), custom_call_target="tpu_custom_call", output_to_operand_aliasing={{0}: (5, {}), {1}: (6, {})} | custom-call | flops 536870912 | bytes 8388608 | tf_op jit(solution)/shard_map/attend/pallas_call | solution.py:290
  (5 shorter events, 0.1 us)
Async XLA Ops:
  0.0 2.8 %copy-start.4 = (bf16[128,2048]{1,0:T(8,128)(2,1)S(1)}, bf16[128,2048]{1,0:T(8,128)(2,1)}, u32[]{:S(2)}) copy-start(bf16[128,2048]{1,0:T(8,128)(2,1)} %own.1) | copy-start | bytes 1572868
  0.0 2.8 %copy-start.5 = (f32[2048]{0:T(1024)S(1)}, f32[2048]{0:T(1024)}, u32[]{:S(2)}) copy-start(f32[2048]{0:T(1024)} %param.9) | copy-start | bytes 24580
  0.0 2.8 %copy-start.2 = (bf16[2048,256]{1,0:T(8,128)(2,1)S(1)}, bf16[2048,256]{1,0:T(8,128)(2,1)}, u32[]{:S(2)}) copy-start(bf16[2048,256]{1,0:T(8,128)(2,1)} %wk.1) | copy-start | bytes 3145732
  0.0 2.8 %copy-start.3 = (bf16[2048,256]{1,0:T(8,128)(2,1)S(1)}, bf16[2048,256]{1,0:T(8,128)(2,1)}, u32[]{:S(2)}) copy-start(bf16[2048,256]{1,0:T(8,128)(2,1)} %wv.1) | copy-start | bytes 3145732
  0.0 2.8 %collective-permute-start = (bf16[128,2048]{1,0:T(8,128)(2,1)}, bf16[128,2048]{1,0:T(8,128)(2,1)S(1)}, u32[]{:S(2)}, u32[]{:S(2)}) collective-permute-start(bf16[128,2048]{1,0:T(8,128)(2,1)} %own.1), channel_id=1, source_target_pairs={{0,1},{1,0},{2,3},{3,2},{4,5},{5,4},{6,7},{7,6},{8,9},{9,8},{10,11... | collective-permute-start | bytes 1572872 | tf_op jit(solution)/shard_map/ppermute | solution.py:327
  0.1 0.8 %copy-start.6 = (s32[32]{0:T(128)S(1)}, s32[32]{0:T(128)}, u32[]{:S(2)}) copy-start(s32[32]{0:T(128)} %lengths.1) | copy-start | bytes 388
  0.9 1.9 %copy-start.7 = (f32[128]{0:T(128)S(1)}, f32[128]{0:T(128)}, u32[]{:S(2)}) copy-start(f32[128]{0:T(128)} %param.14) | copy-start | bytes 1540
  2.8 26.5 %copy-start = (bf16[2048,2048]{1,0:T(8,128)(2,1)S(1)}, bf16[2048,2048]{1,0:T(8,128)(2,1)}, u32[]{:S(2)}) copy-start(bf16[2048,2048]{1,0:T(8,128)(2,1)} %wq.1) | copy-start | bytes 25165828
  2.9 26.5 %copy-start.1 = (f32[128]{0:T(128)S(1)}, f32[128]{0:T(128)}, u32[]{:S(2)}) copy-start(f32[128]{0:T(128)} %param.13) | copy-start | bytes 1540
  4.1 8.7 %collective-permute-start.1 = (bf16[512,256]{1,0:T(8,128)(2,1)S(1)}, bf16[512,256]{1,0:T(8,128)(2,1)S(1)}, u32[]{:S(2)}, u32[]{:S(2)}) collective-permute-start(bf16[512,256]{1,0:T(8,128)(2,1)S(1)} %get-tuple-element.29.refs_0_), channel_id=1, source_target_pairs={{0,8},{2,10},{4,12},{6,14},{8,16},{10,18},{12,20},{14,22},{16,24},... | collective-permute-start | bytes 786440 | tf_op jit(solution)/shard_map/ppermute | solution.py:392
  4.2 15.9 %collective-permute-start.15 = (bf16[512,256]{1,0:T(8,128)(2,1)S(1)}, bf16[512,256]{1,0:T(8,128)(2,1)S(1)}, u32[]{:S(2)}, u32[]{:S(2)}) collective-permute-start(bf16[512,256]{1,0:T(8,128)(2,1)S(1)} %get-tuple-element.29.refs_0_), channel_id=1, source_target_pairs={{0,2},{2,4},{4,6},{6,0},{8,10},{10,12},{12,14},{14,8},{16,18},{18,... | collective-permute-start | bytes 786440 | tf_op jit(solution)/shard_map/ppermute | solution.py:392
  12.8 9.1 %collective-permute-start.2 = (bf16[512,256]{1,0:T(8,128)(2,1)S(1)}, bf16[512,256]{1,0:T(8,128)(2,1)S(1)}, u32[]{:S(2)}, u32[]{:S(2)}) collective-permute-start(bf16[512,256]{1,0:T(8,128)(2,1)S(1)} %collective-permute-done.1.refs_2_), channel_id=1, source_target_pairs={{0,8},{2,10},{4,12},{6,14},{8,16},{10,18},{12,20},{14,22},{16,24},... | collective-permute-start | bytes 786440 | tf_op jit(solution)/shard_map/ppermute | solution.py:392
  16.4 23.7 %collective-permute-start.17 = (bf16[512,256]{1,0:T(8,128)(2,1)S(1)}, bf16[512,256]{1,0:T(8,128)(2,1)S(1)}, u32[]{:S(2)}, u32[]{:S(2)}) collective-permute-start(bf16[512,256]{1,0:T(8,128)(2,1)S(1)} %get-tuple-element.29.refs_0_), channel_id=1, source_target_pairs={{0,6},{2,0},{4,2},{6,4},{8,14},{10,8},{12,10},{14,12},{16,22},{18,... | collective-permute-start | bytes 786440 | tf_op jit(solution)/shard_map/ppermute | solution.py:392
  19.4 12.7 %collective-permute-start.13 = (bf16[512,256]{1,0:T(8,128)(2,1)S(1)}, bf16[512,256]{1,0:T(8,128)(2,1)S(1)}, u32[]{:S(2)}, u32[]{:S(2)}) collective-permute-start(bf16[512,256]{1,0:T(8,128)(2,1)S(1)} %collective-permute-done.1.refs_2_), channel_id=1, source_target_pairs={{0,6},{2,0},{4,2},{6,4},{8,14},{10,8},{12,10},{14,12},{16,22},{18,... | collective-permute-start | bytes 786440 | tf_op jit(solution)/shard_map/ppermute | solution.py:392
  20.2 25.6 %collective-permute-start.16 = (bf16[1024,256]{1,0:T(8,128)(2,1)S(1)}, bf16[1024,256]{1,0:T(8,128)(2,1)S(1)}, u32[]{:S(2)}, u32[]{:S(2)}) collective-permute-start(bf16[1024,256]{1,0:T(8,128)(2,1)S(1)} %pad_maximum_fusion.2), channel_id=1, source_target_pairs={{0,2},{2,4},{4,6},{6,0},{8,10},{10,12},{12,14},{14,8},{16,18},{18,... | collective-permute-start | bytes 1572872 | tf_op jit(solution)/shard_map/ppermute | solution.py:392
  22.0 14.7 %collective-permute-start.3 = (bf16[512,256]{1,0:T(8,128)(2,1)S(1)}, bf16[512,256]{1,0:T(8,128)(2,1)S(1)}, u32[]{:S(2)}, u32[]{:S(2)}) collective-permute-start(bf16[512,256]{1,0:T(8,128)(2,1)S(1)} %collective-permute-done.2.refs_3_), channel_id=1, source_target_pairs={{0,8},{2,10},{4,12},{6,14},{8,16},{10,18},{12,20},{14,22},{16,24},... | collective-permute-start | bytes 786440 | tf_op jit(solution)/shard_map/ppermute | solution.py:392
  27.8 12.1 %collective-permute-start.11 = (bf16[512,256]{1,0:T(8,128)(2,1)S(1)}, bf16[512,256]{1,0:T(8,128)(2,1)S(1)}, u32[]{:S(2)}, u32[]{:S(2)}) collective-permute-start(bf16[512,256]{1,0:T(8,128)(2,1)S(1)} %collective-permute-done.2.refs_3_), channel_id=1, source_target_pairs={{0,2},{2,4},{4,6},{6,0},{8,10},{10,12},{12,14},{14,8},{16,18},{18,... | collective-permute-start | bytes 786440 | tf_op jit(solution)/shard_map/ppermute | solution.py:392
  32.2 25.7 %collective-permute-start.14 = (bf16[1024,256]{1,0:T(8,128)(2,1)S(1)}, bf16[1024,256]{1,0:T(8,128)(2,1)S(1)}, u32[]{:S(2)}, u32[]{:S(2)}) collective-permute-start(bf16[1024,256]{1,0:T(8,128)(2,1)S(1)} %pad_maximum_fusion.1), channel_id=1, source_target_pairs={{0,6},{2,0},{4,2},{6,4},{8,14},{10,8},{12,10},{14,12},{16,22},{18,... | collective-permute-start | bytes 1572872 | tf_op jit(solution)/shard_map/ppermute | solution.py:392
  36.7 8.7 %collective-permute-start.4 = (bf16[512,256]{1,0:T(8,128)(2,1)S(1)}, bf16[512,256]{1,0:T(8,128)(2,1)S(1)}, u32[]{:S(2)}, u32[]{:S(2)}) collective-permute-start(bf16[512,256]{1,0:T(8,128)(2,1)S(1)} %collective-permute-done.3.refs_3_), channel_id=1, source_target_pairs={{0,8},{2,10},{4,12},{6,14},{8,16},{10,18},{12,20},{14,22},{16,24},... | collective-permute-start | bytes 786440 | tf_op jit(solution)/shard_map/ppermute | solution.py:392
  39.9 28.0 %collective-permute-start.12 = (bf16[1024,256]{1,0:T(8,128)(2,1)S(1)}, bf16[1024,256]{1,0:T(8,128)(2,1)S(1)}, u32[]{:S(2)}, u32[]{:S(2)}) collective-permute-start(bf16[1024,256]{1,0:T(8,128)(2,1)S(1)} %pad_maximum_fusion), channel_id=1, source_target_pairs={{0,2},{2,4},{4,6},{6,0},{8,10},{10,12},{12,14},{14,8},{16,18},{18,... | collective-permute-start | bytes 1572872 | tf_op jit(solution)/shard_map/ppermute | solution.py:392
  40.1 13.9 %collective-permute-start.9 = (bf16[512,256]{1,0:T(8,128)(2,1)S(1)}, bf16[512,256]{1,0:T(8,128)(2,1)S(1)}, u32[]{:S(2)}, u32[]{:S(2)}) collective-permute-start(bf16[512,256]{1,0:T(8,128)(2,1)S(1)} %collective-permute-done.3.refs_3_), channel_id=1, source_target_pairs={{0,6},{2,0},{4,2},{6,4},{8,14},{10,8},{12,10},{14,12},{16,22},{18,... | collective-permute-start | bytes 786440 | tf_op jit(solution)/shard_map/ppermute | solution.py:392
  45.4 19.1 %collective-permute-start.5 = (bf16[512,256]{1,0:T(8,128)(2,1)S(1)}, bf16[512,256]{1,0:T(8,128)(2,1)S(1)}, u32[]{:S(2)}, u32[]{:S(2)}) collective-permute-start(bf16[512,256]{1,0:T(8,128)(2,1)S(1)} %collective-permute-done.4.refs_3_), channel_id=1, source_target_pairs={{0,2},{2,4},{4,6},{6,0},{8,10},{10,12},{12,14},{14,8},{16,18},{18,... | collective-permute-start | bytes 786440 | tf_op jit(solution)/shard_map/ppermute | solution.py:392
  45.9 18.7 %collective-permute-start.7 = (bf16[512,256]{1,0:T(8,128)(2,1)S(1)}, bf16[512,256]{1,0:T(8,128)(2,1)S(1)}, u32[]{:S(2)}, u32[]{:S(2)}) collective-permute-start(bf16[512,256]{1,0:T(8,128)(2,1)S(1)} %collective-permute-done.4.refs_3_), channel_id=1, source_target_pairs={{0,6},{2,0},{4,2},{6,4},{8,14},{10,8},{12,10},{14,12},{16,22},{18,... | collective-permute-start | bytes 786440 | tf_op jit(solution)/shard_map/ppermute | solution.py:392
  54.0 19.0 %collective-permute-start.10 = (bf16[512,256]{1,0:T(8,128)(2,1)S(1)}, bf16[512,256]{1,0:T(8,128)(2,1)S(1)}, u32[]{:S(2)}, u32[]{:S(2)}) collective-permute-start(bf16[512,256]{1,0:T(8,128)(2,1)S(1)} %collective-permute-done.9.refs_2_), channel_id=1, source_target_pairs={{0,6},{2,0},{4,2},{6,4},{8,14},{10,8},{12,10},{14,12},{16,22},{18,... | collective-permute-start | bytes 786440 | tf_op jit(solution)/shard_map/ppermute | solution.py:392
  64.5 12.5 %collective-permute-start.6 = (bf16[256,256]{1,0:T(8,128)(2,1)S(1)}, bf16[256,256]{1,0:T(8,128)(2,1)S(1)}, u32[]{:S(2)}, u32[]{:S(2)}) collective-permute-start(bf16[256,256]{1,0:T(8,128)(2,1)S(1)} %slice.8), channel_id=1, source_target_pairs={{0,2},{2,4},{4,6},{6,0},{8,10},{10,12},{12,14},{14,8},{16,18},{18,... | collective-permute-start | bytes 393224 | tf_op jit(solution)/shard_map/ppermute | solution.py:392
  64.6 12.3 %collective-permute-start.8 = (bf16[256,256]{1,0:T(8,128)(2,1)S(1)}, bf16[256,256]{1,0:T(8,128)(2,1)S(1)}, u32[]{:S(2)}, u32[]{:S(2)}) collective-permute-start(bf16[256,256]{1,0:T(8,128)(2,1)S(1)} %slice.9), channel_id=1, source_target_pairs={{0,6},{2,0},{4,2},{6,4},{8,14},{10,8},{12,10},{14,12},{16,22},{18,... | collective-permute-start | bytes 393224 | tf_op jit(solution)/shard_map/ppermute | solution.py:392
